TPU v7x, 256 devices: a whole 4x4x8 slice. The times are simulated.
256 devices in a mesh: gx: 4 (over y_lo, core), gy: 8 (over x, y_hi), gz: 8 (over z).
Axes of the slice: x: 4, y: 4 (y_hi: 2, y_lo: 2; y = y_hi * 2 + y_lo), z: 8, core: 2. Of those that a mesh axis runs over, the one named last changes fastest.
Arguments:
- tokens: bfloat16 [32, 64, 64, 256], P('gx', 'gy', 'gz'), may hold values from -6 to 6
- norm_gain: float32 [256], replicated, may hold values from 0.5 to 1.5
- query_weight: bfloat16 [256, 256], replicated, may hold values from -2 to 2
- key_weight: bfloat16 [256, 256], replicated, may hold values from -2 to 2
- value_weight: bfloat16 [256, 256], replicated, may hold values from -0.375 to 0.375
- head_scale: float32 [8], replicated, may hold values from 1 to 6
- out_weight: bfloat16 [256, 256], replicated, may hold values from -0.375 to 0.375
- mlp_gain: float32 [256], replicated, may hold values from 0.5 to 1.5
- up_weight: bfloat16 [256, 512], replicated, may hold values from -0.375 to 0.375
- down_weight: bfloat16 [512, 256], replicated, may hold values from -0.25 to 0.25
Outputs:
- layer_out: bfloat16 [32, 64, 64, 256], P('gx', 'gy', 'gz')
All inputs are finite; a program needn't handle non-finite values.
Results may differ from a plain program's by a relative error of at most 0.0095.
Values may be sent and summed in bfloat16 or wider, within the bound.
A program may use at most 128 MiB of HBM per device.

v0:
```python
import math

import jax
import jax.numpy as jnp
from jax import lax
from jax.sharding import PartitionSpec as P

HEADS = 8


EPSILON = 1e-05


def extended(cells, sides, width):
    for axis, dim in sides:
        count = lax.axis_size(axis)
        head = lax.slice_in_dim(cells, 0, width, axis=dim)
        tail = lax.slice_in_dim(cells, cells.shape[dim] - width, cells.shape[dim], axis=dim)
        cells = jnp.concatenate(
            [
                lax.ppermute(tail, axis, [(i, (i + 1) % count) for i in range(count)]),
                cells,
                lax.ppermute(head, axis, [((i + 1) % count, i) for i in range(count)]),
            ],
            axis=dim,
        )
    return cells


def layer_norm(values, gain):
    widened = values.astype(jnp.float32)
    average = jnp.mean(widened, axis=-1, keepdims=True)
    centered = widened - average
    variance = jnp.mean(centered * centered, axis=-1, keepdims=True)
    return (centered * lax.rsqrt(variance + EPSILON) * gain).astype(jnp.bfloat16)


def project(values, weight):
    flat = values.reshape(-1, values.shape[-1])
    result = jnp.dot(flat, weight, preferred_element_type=jnp.float32)
    return result.astype(jnp.bfloat16).reshape(values.shape[:-1] + (weight.shape[1],))


def pooled_mean(values, factor):
    extent = values.shape
    grouped = values.reshape(
        extent[0] // factor,
        factor,
        extent[1] // factor,
        factor,
        extent[2] // factor,
        factor,
        extent[3],
    )
    return jnp.mean(grouped, axis=(1, 3, 5), dtype=jnp.float32).astype(jnp.bfloat16)


def unfold_axis(padded, dimension):
    windows = padded.shape[dimension] // 2 - 1
    paired = padded.reshape(
        padded.shape[:dimension] + (windows + 1, 2) + padded.shape[dimension + 1 :]
    )
    lower = lax.slice_in_dim(paired, 0, windows, axis=dimension)
    upper = lax.slice_in_dim(paired, 1, windows + 1, axis=dimension)
    return jnp.concatenate([lower, upper], axis=dimension + 1)


def unfold(padded):
    for dimension in (0, 2, 4):
        padded = unfold_axis(padded, dimension)
    return padded.transpose(0, 2, 4, 1, 3, 5, 6).reshape(
        padded.shape[0], padded.shape[2], padded.shape[4], 64, padded.shape[6]
    )


def window_attend(key_pad, value_pad, queries, scaling):
    key_cells = unfold(key_pad)
    value_cells = unfold(value_pad)
    along_x, along_y, along_z, window_size, channels = key_cells.shape
    head_width = channels // HEADS
    query_side = queries.shape[0] // along_x
    windows = along_x * along_y * along_z
    grouped = queries.reshape(
        along_x, query_side, along_y, query_side, along_z, query_side, channels
    )
    grouped = grouped.transpose(0, 2, 4, 1, 3, 5, 6).reshape(
        windows, query_side**3, HEADS, head_width
    )
    key_cells = key_cells.reshape(windows, window_size, HEADS, head_width)
    value_cells = value_cells.reshape(windows, window_size, HEADS, head_width)
    scores = (
        jnp.einsum("wqhd,wkhd->whqk", grouped, key_cells, preferred_element_type=jnp.float32)
        * scaling[None, :, None, None]
    )
    highest = jnp.max(scores, axis=-1, keepdims=True)
    weights = jnp.exp(scores - highest)
    summed = jnp.sum(weights, axis=-1, keepdims=True)
    blended = jnp.einsum(
        "whqk,wkhd->wqhd",
        weights.astype(jnp.bfloat16),
        value_cells,
        preferred_element_type=jnp.float32,
    )
    blended = blended / jnp.transpose(summed, (0, 2, 1, 3))
    blended = blended.reshape(
        along_x, along_y, along_z, query_side, query_side, query_side, channels
    )
    return blended.transpose(0, 3, 1, 4, 2, 5, 6).reshape(queries.shape)


def absorb(running, key_cells, value_cells, query_heads, scaling):
    highest, summed, collected = running
    head_width = query_heads.shape[-1]
    key_heads = key_cells.reshape(-1, HEADS, head_width)
    value_heads = value_cells.reshape(-1, HEADS, head_width)
    scores = (
        jnp.einsum("qhd,khd->hqk", query_heads, key_heads, preferred_element_type=jnp.float32)
        * scaling[:, None, None]
    )
    raised = jnp.maximum(highest, jnp.max(scores, axis=-1))
    shrink = jnp.exp(highest - raised)
    weights = jnp.exp(scores - raised[:, :, None])
    summed = summed * shrink + jnp.sum(weights, axis=-1)
    collected = collected * jnp.transpose(shrink)[:, :, None] + jnp.einsum(
        "hqk,khd->qhd",
        weights.astype(jnp.bfloat16),
        value_heads,
        preferred_element_type=jnp.float32,
    )
    return (raised, summed, collected)


def fold_keys(running, key_cells, value_cells, query_heads, scaling):
    total_keys = key_cells.shape[0]

    def one_block(block_index, partial_state):
        opening = block_index * 512
        key_block = lax.dynamic_slice_in_dim(key_cells, opening, 512, 0)
        value_block = lax.dynamic_slice_in_dim(value_cells, opening, 512, 0)
        return absorb(partial_state, key_block, value_block, query_heads, scaling)

    return lax.fori_loop(0, total_keys // 512, one_block, running)


def shards(
    tokens,
    norm_gain,
    query_weight,
    key_weight,
    value_weight,
    head_scale,
    out_weight,
    mlp_gain,
    up_weight,
    down_weight,
):
    channels = tokens.shape[-1]
    head_width = channels // HEADS
    scaling = head_scale / math.sqrt(head_width)
    normed = layer_norm(tokens, norm_gain)
    queries = project(normed, query_weight)
    fine_pair = jnp.stack([project(normed, key_weight), project(normed, value_weight)])
    fine_pad = extended(fine_pair, (("gx", 1), ("gy", 2), ("gz", 3)), 1)
    key_pad, value_pad = (fine_pad[0], fine_pad[1])
    middle = pooled_mean(normed, 2)
    middle_pair = jnp.stack([project(middle, key_weight), project(middle, value_weight)])
    middle_pad = extended(middle_pair, (("gx", 1), ("gy", 2), ("gz", 3)), 1)
    middle_key_pad, middle_value_pad = (middle_pad[0], middle_pad[1])
    fine_out = window_attend(key_pad, value_pad, queries, scaling)
    middle_out = window_attend(middle_key_pad, middle_value_pad, queries, scaling)
    coarse = pooled_mean(normed, 4).reshape(-1, channels)
    query_heads = queries.reshape(-1, HEADS, head_width)
    rows_here = query_heads.shape[0]
    initial = (
        jnp.full((HEADS, rows_here), -1e30, jnp.float32),
        jnp.zeros((HEADS, rows_here), jnp.float32),
        jnp.zeros((rows_here, HEADS, head_width), jnp.float32),
    )
    portion = lax.all_gather(coarse, ("gx", "gy", "gz"), axis=0, tiled=True)
    running = fold_keys(
        initial, project(portion, key_weight), project(portion, value_weight), query_heads, scaling
    )
    coarse_out = (running[2] / jnp.transpose(running[1])[:, :, None]).reshape(tokens.shape)
    attended = (fine_out + middle_out + coarse_out).astype(jnp.bfloat16)
    flat_tokens = tokens.reshape(-1, channels)
    residual = (
        flat_tokens.astype(jnp.float32)
        + jnp.dot(attended.reshape(-1, channels), out_weight, preferred_element_type=jnp.float32)
    ).astype(jnp.bfloat16)
    second = layer_norm(residual, mlp_gain)
    hidden = jax.nn.gelu(
        jnp.dot(second, up_weight, preferred_element_type=jnp.float32), approximate=True
    ).astype(jnp.bfloat16)
    output = residual.astype(jnp.float32) + jnp.dot(
        hidden, down_weight, preferred_element_type=jnp.float32
    )
    return output.astype(jnp.bfloat16).reshape(tokens.shape)


def solution(mesh):
    in_specs = (P("gx", "gy", "gz", None), P(), P(), P(), P(), P(), P(), P(), P(), P())
    out_specs = P("gx", "gy", "gz", None)
    return jax.shard_map(shards, mesh=mesh, in_specs=in_specs, out_specs=out_specs, check_vma=False)
```

profile of v0, /device:TPU:1, one launch (start us, length us, event | category | flops | bytes accessed | tf_op | source)
XLA Modules:
  0.0 632.0 jit_solution(17958649177231556539)
XLA Ops:
  11.3 2.8 collective-permute-start.6
  19.1 2.2 collective-permute-start.8
  21.3 3.0 collective-permute-start.9
  25.3 1.4 reshape.147
  28.8 4.0 collective-permute-start.11
  34.4 4.8 collective-permute-start.3
  41.8 1.4 reshape_reshape.26
  45.5 1.9 multiply_reduce_fusion
  47.4 1.3 copy-done.3
  49.7 1.4 reshape_reshape.24
  51.1 1.7 pad_maximum_fusion.10
  52.8 2.7 collective-permute-start.5
  55.5 3.5 fusion.23
  59.0 3.2 copy.63
  62.2 2.4 reshape.149
  65.4 2.0 reshape.150
  67.5 1.9 pad_maximum_fusion
  74.6 2.1 fusion.69
  80.7 2.1 fusion.70
  82.9 1.4 maximum_bitcast_fusion.1
  84.2 2.7 copy.46
  86.9 10.4 %reshape_reshape.23 = bf16[64,64,8,32]{3,2,1,0:T(8,128)(2,1)} reshape(bf16[4,4,4,4,4,4,256]{6,5,4,3,2,1,0:T(4,128)(2,1)} %copy.46) | data formatting | bytes 4194304 | tf_op jit(solution)/shard_map/reshape;reshape | solution.py:89
  97.4 2.9 maximum_bitcast_fusion
  100.3 2.7 copy.43
  102.9 10.2 %reshape_reshape.21 = bf16[64,64,8,32]{3,2,1,0:T(8,128)(2,1)} reshape(bf16[4,4,4,4,4,4,256]{6,5,4,3,2,1,0:T(4,128)(2,1)} %copy.43) | data formatting | bytes 4194304 | tf_op jit(solution)/shard_map/reshape;reshape | solution.py:90
  113.1 7.1 %multiply_reduce_fusion.1 = (f32[64,8,8]{2,1,0:T(8,128)S(1)}, f32[64,8,8,64]{3,2,1,0:T(8,128)S(1)}) fusion(f32[8]{0:T(128)S(1)} %copy-done.24, bf16[64,64,8,32]{3,2,1,0:T(8,128)(2,1)} %reshape_reshape.23, bf16[64,8,8,32]{3,2,1,0:T(8,128)(2,1)S(1)} %reshape.142), kind=kOutput, calls=%fused_computation.28 | convolution fusion | flops 17297408 | bytes 3424288 | tf_op jit(solution)/shard_map/wqhd,wkhd->whqk/dot_general | solution.py:92
  120.2 1.4 copy-done.4
  121.6 1.3 fusion.17
  122.9 5.2 bitcast_divide_fusion
  128.1 3.4 copy.50
  131.5 2.4 reshape.144
  134.6 424.2 %all-gather.2.cloned.1.call-done = bf16[2048,256]{1,0:T(8,128)(2,1)} async-done(((bf16[8,256]{1,0:T(8,128)(2,1)}), bf16[2048,256]{1,0:T(8,128)(2,1)}) %all-gather.2.cloned.1.call-update) | async-done | bytes 1048592 | tf_op jit(solution)/shard_map/all_gather | solution.py:179
  558.9 1.7 convolution_convert_fusion
  560.6 1.5 convolution_convert_fusion.1
  562.1 58.5 %while.18 = (s32[]{:T(128)}, f32[8,512]{1,0:T(8,128)S(1)}, f32[8,512]{1,0:T(8,128)}, f32[512,8,32]{0,2,1:T(8,128)S(1)}, bf16[2048,256]{1,0:T(8,128)(2,1)}, /*ind...) while((s32[]{:T(128)}, f32[8,512]{1,0:T(8,128)S(1)}, ...), condition=%wide.region_11.0_spmd.clone, body=%wide.region_8.0_spmd.clone.sunk | while | flops 285630464 | bytes 63046152 | solution.py:142
  563.5 5.4 bitcast_reduce_fusion.2
  569.1 5.1 fusion.112
  574.9 1.4 fusion.110
  578.1 5.4 bitcast_reduce_fusion.2
  583.7 5.1 fusion.112
  589.4 1.4 fusion.110
  592.7 5.4 bitcast_reduce_fusion.2
  598.2 5.1 fusion.112
  604.0 1.4 fusion.110
  607.2 5.4 bitcast_reduce_fusion.2
  612.8 5.1 fusion.112
  618.6 1.4 fusion.110
  622.4 2.3 fusion.26
  (208 shorter events, 42.3 us)
Async XLA Ops:
  6.5 615.9 %copy-start = (bf16[512,256]{1,0:T(8,128)(2,1)S(1)}, bf16[512,256]{1,0:T(8,128)(2,1)}, u32[]{:S(2)}) copy-start(bf16[512,256]{1,0:T(8,128)(2,1)} %param.21) | copy-start | bytes 786436
  6.5 4.2 copy-start.13
  6.5 4.4 copy-start.12
  6.5 552.3 %all-gather.2.cloned.1.call-start = ((), (), s32[]{:S(2)}) async-start(), calls=%async_computation | async-start | bytes 1052672 | tf_op jit(solution)/shard_map/all_gather | solution.py:179
  11.3 7.8 %collective-permute-start.6 = (bf16[2,1,4,4,256]{4,1,3,2,0:T(2,128)(2,1)S(1)}, bf16[2,1,4,4,256]{4,1,3,2,0:T(2,128)(2,1)S(1)}, u32[]{:S(2)}, u32[]{:S(2)}) collective-permute-start(bf16[2,1,4,4,256]{4,1,3,2,0:T(2,128)(2,1)S(1)} %get-tuple-element.246), channel_id=1, source_target_pairs={{0,64},{64,128},{128,192},{192,0},{1,65},{65,129},{129,193},{193,1... | collective-permute-start | bytes 49160 | tf_op jit(solution)/shard_map/ppermute | solution.py:21
  14.0 5.1 collective-permute-start.7
  14.6 4.2 copy-start.26
  14.9 9.4 %copy-start.31 = (f32[8]{0:T(128)S(1)}, f32[8]{0:T(128)}, u32[]{:S(2)}) copy-start(f32[8]{0:T(128)} %param.17) | copy-start | bytes 100
  16.3 16.5 %collective-permute-start = (bf16[2,1,8,8,256]{4,1,3,2,0:T(2,128)(2,1)}, bf16[2,1,8,8,256]{4,1,3,2,0:T(2,128)(2,1)S(1)}, u32[]{:S(2)}, u32[]{:S(2)}) collective-permute-start(bf16[2,1,8,8,256]{4,1,3,2,0:T(2,128)(2,1)} %get-tuple-element.232), channel_id=1, source_target_pairs={{0,64},{64,128},{128,192},{192,0},{1,65},{65,129},{129,193},{193,1... | collective-permute-start | bytes 196616 | tf_op jit(solution)/shard_map/ppermute | solution.py:21
  17.4 15.4 %collective-permute-start.1 = (bf16[2,1,8,8,256]{4,1,3,2,0:T(2,128)(2,1)}, bf16[2,1,8,8,256]{4,1,3,2,0:T(2,128)(2,1)S(1)}, u32[]{:S(2)}, u32[]{:S(2)}) collective-permute-start(bf16[2,1,8,8,256]{4,1,3,2,0:T(2,128)(2,1)} %get-tuple-element.233), channel_id=1, source_target_pairs={{64,0},{128,64},{192,128},{0,192},{65,1},{129,65},{193,129},{1,193... | collective-permute-start | bytes 196616 | tf_op jit(solution)/shard_map/ppermute | solution.py:23
  19.1 8.4 %copy-start.22 = (bf16[2,1,4,4,256]{4,1,3,2,0:T(2,128)(2,1)}, bf16[2,1,4,4,256]{4,1,3,2,0:T(2,128)(2,1)S(1)}, u32[]{:S(2)}) copy-start(bf16[2,1,4,4,256]{4,1,3,2,0:T(2,128)(2,1)S(1)} %collective-permute-done.7) | copy-start | bytes 49156
  19.1 8.3 %collective-permute-start.8 = (bf16[2,6,1,4,256]{4,1,3,2,0:T(8,128)(2,1)S(1)}, bf16[2,6,1,4,256]{4,1,3,2,0:T(8,128)(2,1)S(1)}, u32[]{:S(2)}, u32[]{:S(2)}) collective-permute-start(bf16[2,6,1,4,256]{4,1,3,2,0:T(8,128)(2,1)S(1)} %get-tuple-element.244), channel_id=1, source_target_pairs={{0,8},{8,16},{16,24},{24,32},{32,40},{40,48},{48,56},{56,0},{1,9},... | collective-permute-start | bytes 73736 | tf_op jit(solution)/shard_map/ppermute | solution.py:21
  21.3 6.2 collective-permute-start.9
  27.5 11.7 %copy-start.28 = (bf16[2,6,1,4,256]{4,1,3,2,0:T(8,128)(2,1)}, bf16[2,6,1,4,256]{4,1,3,2,0:T(8,128)(2,1)S(1)}, u32[]{:S(2)}) copy-start(bf16[2,6,1,4,256]{4,1,3,2,0:T(8,128)(2,1)S(1)} %collective-permute-done.8) | copy-start | bytes 73732
  27.5 11.7 %copy-start.29 = (bf16[2,6,1,4,256]{4,1,3,2,0:T(8,128)(2,1)}, bf16[2,6,1,4,256]{4,1,3,2,0:T(8,128)(2,1)S(1)}, u32[]{:S(2)}) copy-start(bf16[2,6,1,4,256]{4,1,3,2,0:T(8,128)(2,1)S(1)} %collective-permute-done.9) | copy-start | bytes 73732
  27.6 11.6 %collective-permute-start.10 = (bf16[2,6,6,1,256]{4,1,3,2,0:T(8,128)(2,1)S(1)}, bf16[2,6,6,1,256]{4,1,3,2,0:T(8,128)(2,1)S(1)}, u32[]{:S(2)}, u32[]{:S(2)}) collective-permute-start(bf16[2,6,6,1,256]{4,1,3,2,0:T(8,128)(2,1)S(1)} %get-tuple-element.242), channel_id=1, source_target_pairs={{0,1},{1,2},{2,3},{3,4},{4,5},{5,6},{6,7},{7,0},{8,9},{9,10},{10,1... | collective-permute-start | bytes 110600 | tf_op jit(solution)/shard_map/ppermute | solution.py:21
  28.8 10.4 %collective-permute-start.11 = (bf16[2,6,6,1,256]{4,1,3,2,0:T(8,128)(2,1)S(1)}, bf16[2,6,6,1,256]{4,1,3,2,0:T(8,128)(2,1)S(1)}, u32[]{:S(2)}, u32[]{:S(2)}) collective-permute-start(bf16[2,6,6,1,256]{4,1,3,2,0:T(8,128)(2,1)S(1)} %get-tuple-element.243), channel_id=1, source_target_pairs={{1,0},{2,1},{3,2},{4,3},{5,4},{6,5},{7,6},{0,7},{9,8},{10,9},{11,1... | collective-permute-start | bytes 110600 | tf_op jit(solution)/shard_map/ppermute | solution.py:23
  32.8 18.3 %copy-start.15 = (bf16[2,1,8,8,256]{4,1,3,2,0:T(2,128)(2,1)}, bf16[2,1,8,8,256]{4,1,3,2,0:T(2,128)(2,1)S(1)}, u32[]{:S(2)}) copy-start(bf16[2,1,8,8,256]{4,1,3,2,0:T(2,128)(2,1)S(1)} %collective-permute-done) | copy-start | bytes 196612
  32.8 6.4 %copy-start.17 = (bf16[2,1,8,8,256]{4,1,3,2,0:T(2,128)(2,1)}, bf16[2,1,8,8,256]{4,1,3,2,0:T(2,128)(2,1)S(1)}, u32[]{:S(2)}) copy-start(bf16[2,1,8,8,256]{4,1,3,2,0:T(2,128)(2,1)S(1)} %collective-permute-done.1) | copy-start | bytes 196612
  33.7 17.4 %collective-permute-start.2 = (bf16[2,10,1,8,256]{4,1,3,2,0:T(8,128)(2,1)}, bf16[2,10,1,8,256]{4,1,3,2,0:T(8,128)(2,1)}, u32[]{:S(2)}, u32[]{:S(2)}) collective-permute-start(bf16[2,10,1,8,256]{4,1,3,2,0:T(8,128)(2,1)} %get-tuple-element.230), channel_id=1, source_target_pairs={{0,8},{8,16},{16,24},{24,32},{32,40},{40,48},{48,56},{56,0},{1,9},... | collective-permute-start | bytes 245768 | tf_op jit(solution)/shard_map/ppermute | solution.py:21
  34.4 16.7 %collective-permute-start.3 = (bf16[2,10,1,8,256]{4,1,3,2,0:T(8,128)(2,1)}, bf16[2,10,1,8,256]{4,1,3,2,0:T(8,128)(2,1)}, u32[]{:S(2)}, u32[]{:S(2)}) collective-permute-start(bf16[2,10,1,8,256]{4,1,3,2,0:T(8,128)(2,1)} %get-tuple-element.231), channel_id=1, source_target_pairs={{8,0},{16,8},{24,16},{32,24},{40,32},{48,40},{56,48},{0,56},{9,1},... | collective-permute-start | bytes 245768 | tf_op jit(solution)/shard_map/ppermute | solution.py:23
  41.0 3.1 copy-start.21
  41.5 3.2 copy-start.23
  47.4 1.4 copy-start.3
  48.7 2.4 copy-start.18
  52.8 14.7 %collective-permute-start.4 = (bf16[2,10,10,1,256]{4,1,3,2,0:T(8,128)(2,1)}, bf16[2,10,10,1,256]{4,1,3,2,0:T(8,128)(2,1)}, u32[]{:S(2)}, u32[]{:S(2)}) collective-permute-start(bf16[2,10,10,1,256]{4,1,3,2,0:T(8,128)(2,1)} %get-tuple-element.228), channel_id=1, source_target_pairs={{0,1},{1,2},{2,3},{3,4},{4,5},{5,6},{6,7},{7,0},{8,9},{9,10},{10,1... | collective-permute-start | bytes 307208 | tf_op jit(solution)/shard_map/ppermute | solution.py:21
  52.8 14.7 %collective-permute-start.5 = (bf16[2,10,10,1,256]{4,1,3,2,0:T(8,128)(2,1)}, bf16[2,10,10,1,256]{4,1,3,2,0:T(8,128)(2,1)}, u32[]{:S(2)}, u32[]{:S(2)}) collective-permute-start(bf16[2,10,10,1,256]{4,1,3,2,0:T(8,128)(2,1)} %get-tuple-element.229), channel_id=1, source_target_pairs={{1,0},{2,1},{3,2},{4,3},{5,4},{6,5},{7,6},{0,7},{9,8},{10,9},{11,1... | collective-permute-start | bytes 307208 | tf_op jit(solution)/shard_map/ppermute | solution.py:23
  62.2 5.3 copy-start.16
  74.6 2.1 copy-start.11
  80.7 2.1 copy-start.8
  80.7 2.1 copy-start.9
  102.9 10.2 %copy-start.24 = (f32[8]{0:T(128)S(1)}, f32[8]{0:T(128)}, u32[]{:S(2)}) copy-start(f32[8]{0:T(128)} %broadcast_multiply_fusion.2) | copy-start | bytes 100
  113.1 9.8 %copy-start.2 = (bf16[64,64,8,32]{3,2,1,0:T(8,128)(2,1)S(1)}, bf16[64,64,8,32]{3,2,1,0:T(8,128)(2,1)}, u32[]{:S(2)}) copy-start(bf16[64,64,8,32]{3,2,1,0:T(8,128)(2,1)} %reshape_reshape.21) | copy-start | bytes 6291460
  120.2 1.4 copy-start.4
  134.0 426.7 %copy-start.14 = (bf16[256,256]{1,0:T(8,128)(2,1)S(1)}, bf16[256,256]{1,0:T(8,128)(2,1)}, u32[]{:S(2)}) copy-start(bf16[256,256]{1,0:T(8,128)(2,1)} %param.15) | copy-start | bytes 393220
  558.9 1.8 copy-start.6
  563.5 5.6 copy-start.25
  569.1 5.8 copy-start.1
  574.9 1.5 copy-start.19
  578.1 5.6 copy-start.25
  583.7 5.8 copy-start.1
  589.4 1.5 copy-start.19
  592.7 5.6 copy-start.25
  598.2 5.8 copy-start.1
  604.0 1.5 copy-start.19
  607.2 5.6 copy-start.25
  612.8 5.8 copy-start.1
  618.6 1.5 copy-start.19
  (9 other events, 7.9 us)
Sparse Core Ops, SparseCore 0:
  18.9 539.9 all-gather.1
where the time goes:
time: 642 us; the launch traced here: 632 us
  waiting for transfers between devices  424 us (66%)
  local copies, waits for them, and re-layouts  74.8 us (12%)
  matrix products  66.7 us (10%)
  other arithmetic  27.4 us (4%)
  starting transfers between devices  23.6 us (4%)
  between operations  14.6 us (2%)
    all_gather x1, waiting for transfers between devices, shards(): portion = lax.all_gather(coarse, ('gx', 'gy', 'gz'), axis=0, tiled=True)  424 us
    dot_general x4, matrix products, absorb(): jnp.einsum('qhd,khd->hqk', query_heads, key_heads, preferred_element_type...  21.6 us
    dot_general x4, matrix products, absorb(): jnp.einsum('hqk,khd->qhd', weights.astype(jnp.bfloat16), value_heads, pre...  20.6 us
    ppermute x6, starting transfers between devices, extended(): lax.ppermute(head, axis, [((i + 1) % count, i) for i in range(count)])  15.6 us
  transfers between devices with their start and end apart: 13, of which 1 were waited for; matrix products, arithmetic and copies ran while one was open for 15% of the time, Pallas kernels for 0%

commit v1 on v0

v1 whole, which is shorter than its diff:
```python
import functools
import math

import jax
import jax.numpy as jnp
import numpy as np
from jax import lax
from jax.experimental import pallas as pl
from jax.experimental.pallas import tpu as pltpu
from jax.sharding import PartitionSpec as P

MESH = pl.DeviceIdType.MESH
BF = jnp.bfloat16
F32 = jnp.float32
HEADS = 8
EPSILON = 1e-05
LOG2E = math.log2(math.e)
NEG = -1e30

FACES = [(1, 0, 0), (-1, 0, 0), (0, 1, 0), (0, -1, 0), (0, 0, 1), (0, 0, -1)]
OTHERS = [
    (i, j, k)
    for i in (1, 0, -1)
    for j in (1, 0, -1)
    for k in (1, 0, -1)
    if abs(i) + abs(j) + abs(k) > 1
]
DIRS = FACES + OTHERS
PACKED = 800
SRC = 1024
MID_AT = 896


def slot(d):
    if d in FACES:
        return 80 * FACES.index(d), 80
    return 512 + 16 * OTHERS.index(d), 16


def packed_slot(d):
    start, rows = slot(d)
    return (start if start < 512 else start - 32), rows


AT_Z, AT_M, AT_MZ, KEYS = 800, 1120, 1312, 1408


def halo_row(x, y, z, n, middle):
    d = tuple(1 if c == 0 else -1 if c == n + 1 else 0 for c in (x, y, z))
    free = [c - 1 for c, e in zip((x, y, z), d) if e == 0]
    if not any(d):
        return MID_AT + (free[0] * n + free[1]) * n + free[2]
    start, rows = slot(d)
    at = 0
    for c in free:
        at = at * n + c
    return start + at + ((64 if rows == 80 else 8) if middle else 0)


def selection():
    pick = np.zeros((KEYS - AT_Z, SRC), np.float32)
    for by in range(4):
        for x in range(10):
            for yy in range(4):
                for s in range(2):
                    row = by * 80 + x * 8 + yy * 2 + s
                    pick[row, halo_row(x, 2 * by + yy, 9 * s, 8, False)] = 1
    for my in range(2):
        for x in range(6):
            for yy in range(4):
                for z in range(4):
                    row = AT_M - AT_Z + my * 96 + x * 16 + yy * 4 + z
                    pick[row, halo_row(x, 2 * my + yy, z + 1, 4, True)] = 1
                for s in range(2):
                    row = AT_MZ - AT_Z + my * 48 + x * 8 + yy * 2 + s
                    pick[row, halo_row(x, 2 * my + yy, 5 * s, 4, True)] = 1
    return pick


def window_mask():
    mask = np.full((8, 256), NEG, np.float32)
    for q in range(8):
        for lane in range(256):
            if lane < 128:
                at, low = lane % 8 + 1, 2 * (q // 2)
            elif lane < 160:
                at, low = 9 * (lane % 2), 2 * (q // 2)
            elif lane < 224:
                at, low = lane % 4 + 1, 2 * (q // 4)
            else:
                at, low = 5 * (lane % 2), 2 * (q // 4)
            if low <= at <= low + 3:
                mask[q, lane] = 0
    return mask


def dot(a, b):
    return jnp.dot(a, b, preferred_element_type=F32)


def dot_t(a, b):
    return lax.dot_general(a, b, (((1,), (1,)), ((), ())), preferred_element_type=F32)


def normalized(values, gain):
    average = jnp.mean(values, axis=-1, keepdims=True)
    centered = values - average
    variance = jnp.mean(centered * centered, axis=-1, keepdims=True)
    return (centered * lax.rsqrt(variance + EPSILON) * gain).astype(BF)


def cf_rows(cf, k):
    return jnp.concatenate([cf[c, pl.ds(k, 8, stride=4), :] for c in range(2)], axis=1)


def layer_kernel(
    tok_ref, gain_ref, wq_ref, wk_ref, wv_ref, scale_ref, wo_hbm, gain2_ref, up_hbm, down_hbm, pick_hbm, mask_ref,
    out_ref,
    nf, mf, tf, cf, stage, packed, src, zbuf, cbuf, abuf, qn, qm, kbuf, vbuf, fm, kc, va, sa, sb, ms, acc,
    wo_ref, up_ref, down_ref, pick_ref, wvt,
    load_sem, halo_send, halo_recv, z_send, z_recv, a_send, a_recv, b_send, b_recv, c_send, c_recv,
):
    gx, gy, gz = lax.axis_index("gx"), lax.axis_index("gy"), lax.axis_index("gz")
    core, ylow = lax.rem(gx, 2), lax.div(gx, 2)
    xpos, yhigh = lax.div(gy, 2), lax.rem(gy, 2)
    ypos = yhigh * 2 + ylow

    def chip(x, y):
        return (lax.rem(y, 2) * 2 + core, x * 2 + lax.div(y, 2), gz)

    near = [
        (lax.rem(gx + d[0] + 4, 4), lax.rem(gy + d[1] + 8, 8), lax.rem(gz + d[2] + 8, 8))
        for d in DIRS
    ]
    along_z = [(gx, gy, lax.rem(gz + k, 8)) for k in range(1, 8)]
    first = [chip(lax.rem(xpos + k * (1 - core), 4), lax.rem(ypos + k * core, 4)) for k in range(1, 4)]
    then = [chip(lax.rem(xpos + k * core, 4), lax.rem(ypos + k * (1 - core), 4)) for k in range(1, 4)]
    partner = (gx + 1 - 2 * core, gy, gz)

    barrier = pltpu.get_barrier_semaphore()
    greeted = near + along_z + first + then
    for peer in greeted:
        pl.semaphore_signal(barrier, inc=1, device_id=peer, device_id_type=MESH)

    loads = [
        pltpu.make_async_copy(a, b, load_sem.at[i])
        for i, (a, b) in enumerate(
            ((pick_hbm, pick_ref), (wo_hbm, wo_ref), (up_hbm, up_ref), (down_hbm, down_ref))
        )
    ]
    for load in loads:
        load.start()

    normed = normalized(tok_ref[...].astype(F32), gain_ref[...])
    widened = normed.astype(F32)
    for c in range(2):
        half = widened[:, c * 128 : c * 128 + 128]
        nf[c] = half
        pairs = jnp.sum(half.reshape(4, 2, 4, 2, 8, 128), axis=(1, 3))
        tf[c] = pairs.reshape(128, 128)
        mf[c] = ((tf[c, pl.ds(0, 64, stride=2), :] + tf[c, pl.ds(1, 64, stride=2), :]) * 0.125).astype(BF).astype(F32)
        cf[c] = jnp.sum(pairs.reshape(2, 2, 2, 2, 8, 128), axis=(1, 3)).reshape(32, 128)
    coarse = cf_rows(cf, 0)
    for k in range(1, 4):
        coarse = coarse + cf_rows(cf, k)
    zbuf[0] = (coarse * (1.0 / 64)).astype(BF)

    for d in DIRS:
        start, rows = packed_slot(d)
        x, y, z = (7 if c > 0 else 0 for c in d)
        mx, my, mz = (3 if c > 0 else 0 for c in d)
        axes = tuple(c != 0 for c in d)
        at = start + (64 if rows == 80 else 8)
        for c in range(2):
            if rows == 16:
                stage[c, start : start + 16, :] = jnp.zeros((16, 128), F32)
            if axes == (True, False, False):
                stage[c, start : start + 64, :] = nf[c, x * 64 : x * 64 + 64, :]
                stage[c, at : at + 16, :] = mf[c, mx * 16 : mx * 16 + 16, :]
            elif axes == (False, True, False):
                for i in range(8):
                    stage[c, start + i * 8 : start + i * 8 + 8, :] = nf[c, i * 64 + y * 8 : i * 64 + y * 8 + 8, :]
                for i in range(4):
                    stage[c, at + i * 4 : at + i * 4 + 4, :] = mf[c, i * 16 + my * 4 : i * 16 + my * 4 + 4, :]
            elif axes == (False, False, True):
                stage[c, start : start + 64, :] = nf[c, pl.ds(z, 64, stride=8), :]
                stage[c, at : at + 16, :] = mf[c, pl.ds(mz, 16, stride=4), :]
            elif axes == (True, True, False):
                stage[c, start : start + 8, :] = nf[c, x * 64 + y * 8 : x * 64 + y * 8 + 8, :]
                stage[c, at : at + 4, :] = mf[c, mx * 16 + my * 4 : mx * 16 + my * 4 + 4, :]
            elif axes == (True, False, True):
                stage[c, start : start + 8, :] = nf[c, pl.ds(x * 64 + z, 8, stride=8), :]
                stage[c, at : at + 4, :] = mf[c, pl.ds(mx * 16 + mz, 4, stride=4), :]
            elif axes == (False, True, True):
                stage[c, start : start + 8, :] = nf[c, pl.ds(y * 8 + z, 8, stride=64), :]
                stage[c, at : at + 4, :] = mf[c, pl.ds(my * 4 + mz, 4, stride=16), :]
            else:
                row, mrow = x * 64 + y * 8 + z, mx * 16 + my * 4 + mz
                stage[c, start : start + 1, :] = nf[c, row : row + 1, :]
                stage[c, at : at + 1, :] = mf[c, mrow : mrow + 1, :]
    packed[...] = jnp.concatenate([stage[0], stage[1]], axis=1).astype(BF)

    src[480:512, :] = jnp.zeros((32, 256), BF)
    src[832:896, :] = jnp.zeros((64, 256), BF)
    src[960:1024, :] = jnp.zeros((64, 256), BF)
    src[MID_AT : MID_AT + 64, :] = jnp.concatenate([mf[0], mf[1]], axis=1).astype(BF)

    pl.semaphore_wait(barrier, len(greeted))

    z_copies = [
        pltpu.make_async_remote_copy(
            src_ref=zbuf.at[0], dst_ref=zbuf.at[k], send_sem=z_send.at[k], recv_sem=z_recv.at[k],
            device_id=along_z[k - 1], device_id_type=MESH,
        )
        for k in range(1, 8)
    ]
    for copy in z_copies:
        copy.start()
    halo = []
    for i, d in enumerate(DIRS):
        start, rows = packed_slot(d)
        land, _ = slot(d)
        halo.append(
            pltpu.make_async_remote_copy(
                src_ref=packed.at[pl.ds(start, rows)], dst_ref=src.at[pl.ds(land, rows)],
                send_sem=halo_send.at[i], recv_sem=halo_recv.at[i], device_id=near[i], device_id_type=MESH,
            )
        )
    for copy in halo:
        copy.start()

    factor = LOG2E / math.sqrt(32)
    lane_head = lax.broadcasted_iota(jnp.int32, (1, 256), 1) // 32
    spread = jnp.zeros((1, 256), F32)
    for h in range(HEADS):
        spread = jnp.where(lane_head == h, scale_ref[h] * factor, spread)
    qn[...] = (dot(normed, wq_ref[...]) * spread).astype(BF)
    turned = dot_t(wq_ref[...].T, normed)
    qm[...] = jnp.zeros_like(qm)
    for h in range(HEADS):
        at = (h % 4) * 32
        qm[h, at : at + 32, :] = (turned[h * 32 : h * 32 + 32, :] * (scale_ref[h] * factor)).astype(BF)
    wvt[...] = wv_ref[...].T
    va[:, 32:48, :] = jnp.ones((HEADS, 16, 256), BF)
    ms[...] = jnp.full_like(ms, NEG)
    acc[...] = jnp.zeros_like(acc)

    for copy in z_copies:
        copy.wait()
    cbuf[0:64, :] = zbuf[...].astype(F32).reshape(64, 256).astype(BF)
    a_copies = [
        pltpu.make_async_remote_copy(
            src_ref=cbuf.at[pl.ds(0, 64)], dst_ref=cbuf.at[pl.ds(64 * k, 64)],
            send_sem=a_send.at[k], recv_sem=a_recv.at[k], device_id=first[k - 1], device_id_type=MESH,
        )
        for k in range(1, 4)
    ]
    for copy in a_copies:
        copy.start()

    for copy in halo:
        copy.wait()

    def cells(d, row):
        start, _ = slot(d)
        at = start + row
        low = at - at % 16
        tile = src[low : low + 16, :].astype(F32)
        return tile[at - low : at - low + 8, :]

    for x in range(10):
        ex = 1 if x == 0 else -1 if x == 9 else 0
        if ex:
            begin, end = cells((ex, 1, 0), 0), cells((ex, -1, 0), 0)
            start, _ = slot((ex, 0, 0))
            inner = src[start : start + 64, :].astype(F32)
        else:
            begin, end = cells((0, 1, 0), (x - 1) * 8), cells((0, -1, 0), (x - 1) * 8)
            own = slice((x - 1) * 64, x * 64)
            inner = jnp.concatenate([nf[0, own, :], nf[1, own, :]], axis=1)
        abuf[x * 80 : x * 80 + 80, :] = jnp.concatenate([begin, inner, end], axis=0).astype(BF)
    loads[0].wait()
    abuf[AT_Z:KEYS, :] = dot(pick_ref[...], src[...]).astype(BF)

    def project(i, carry):
        rows = pl.ds(pl.multiple_of(i * 128, 128), 128)
        a = abuf[rows, :]
        kbuf[rows, :] = dot(a, wk_ref[...]).astype(BF)
        vbuf[rows, :] = dot(a, wv_ref[...]).astype(BF)
        return carry

    lax.fori_loop(0, KEYS // 128, project, 0)

    for copy in a_copies:
        copy.wait()
    b_copies = [
        pltpu.make_async_remote_copy(
            src_ref=cbuf.at[pl.ds(0, 256)], dst_ref=cbuf.at[pl.ds(256 * k, 256)],
            send_sem=b_send.at[k], recv_sem=b_recv.at[k], device_id=then[k - 1], device_id_type=MESH,
        )
        for k in range(1, 4)
    ]
    for copy in b_copies:
        copy.start()
    c_copies = [
        pltpu.make_async_remote_copy(
            src_ref=cbuf.at[pl.ds(256 * k, 256)], dst_ref=cbuf.at[pl.ds(1024 + 256 * k, 256)],
            send_sem=c_send.at[k], recv_sem=c_recv.at[k], device_id=partner, device_id_type=MESH,
        )
        for k in range(4)
    ]
    c_copies[0].start()

    lane = lax.broadcasted_iota(jnp.int32, (1, 128), 1)
    is_fine = lane < 32

    def windows(g, carry):
        bx, by = lax.div(g, 4), lax.rem(g, 4)
        mx, my = lax.div(bx, 2), lax.div(by, 2)

        def rows(start, count):
            return pl.ds(pl.multiple_of(start, 16), count)

        r0 = rows(bx * 128 + by * 16, 16)
        r1 = rows(bx * 128 + by * 16 + 64, 16)
        parts = [rows((2 * bx + i) * 80 + by * 16, 32) for i in range(4)] + [
            rows(AT_Z + by * 80 + bx * 16, 32),
            rows(AT_M + my * 96 + mx * 32, 64),
            rows(AT_MZ + my * 48 + mx * 16, 32),
        ]
        q = jnp.concatenate([qn[r0, :], qn[r1, :]], axis=0)
        spread_q = jnp.concatenate(
            [jnp.where(lane_head == h, q, jnp.zeros_like(q)) for h in range(HEADS)], axis=0
        )
        keys = jnp.concatenate([kbuf[p, :] for p in parts], axis=0)
        values = jnp.concatenate([vbuf[p, :] for p in parts], axis=0)
        scores = (dot_t(spread_q, keys).reshape(32, 8, 256) + mask_ref[...][None]).reshape(256, 256)
        s0, s1 = scores[:, :128], scores[:, 128:]
        top_f = jnp.max(jnp.maximum(s0, jnp.where(is_fine, s1, NEG)), axis=1, keepdims=True)
        top_m = jnp.max(jnp.where(is_fine, NEG, s1), axis=1, keepdims=True)
        e0 = jnp.exp2(s0 - top_f)
        e1 = jnp.exp2(s1 - jnp.where(is_fine, top_f, top_m))
        sum_f = jnp.sum(e0 + jnp.where(is_fine, e1, 0.0), axis=1, keepdims=True)
        sum_m = jnp.sum(jnp.where(is_fine, 0.0, e1), axis=1, keepdims=True)
        inv_f, inv_m = 1.0 / sum_f, 1.0 / sum_m
        weights = jnp.concatenate([e0 * inv_f, e1 * jnp.where(is_fine, inv_f, inv_m)], axis=1).astype(BF)
        mixed = dot(weights, values)
        total = jnp.zeros((32, 256), F32)
        for h in range(HEADS):
            total = jnp.where(lane_head == h, mixed[h * 32 : h * 32 + 32, :], total)
        fm[r0, :] = total[:16]
        fm[r1, :] = total[16:]
        return carry

    lax.fori_loop(0, 16, windows, 0)

    def scores_of(h, into):
        s = dot(kc[h // 4], qm[h])
        into[...] = s
        return jnp.max(s, axis=0, keepdims=True)

    def absorb(h, held, block_top):
        old = ms[h : h + 1, :]
        top = jnp.maximum(old, block_top)
        p = jnp.exp2(held[...] - top).astype(BF)
        acc[h] = acc[h] * jnp.exp2(old - top) + dot(va[h], p)
        ms[h : h + 1, :] = top

    def coarse_block(j, carry):
        s, other = lax.div(j, 2), lax.rem(j, 2)

        @pl.when(jnp.logical_and(other == 0, s > 0))
        def _():
            row = pl.multiple_of(256 * s, 256)
            pltpu.make_async_remote_copy(
                src_ref=cbuf.at[pl.ds(0, 256)], dst_ref=cbuf.at[pl.ds(row, 256)],
                send_sem=b_send.at[s], recv_sem=b_recv.at[s], device_id=then[0], device_id_type=MESH,
            ).wait_recv()
            pltpu.make_async_remote_copy(
                src_ref=cbuf.at[pl.ds(row, 256)], dst_ref=cbuf.at[pl.ds(1024 + row, 256)],
                send_sem=c_send.at[s], recv_sem=c_recv.at[s], device_id=partner, device_id_type=MESH,
            ).start()

        @pl.when(other == 1)
        def _():
            row = pl.multiple_of(256 * s, 256)
            pltpu.make_async_remote_copy(
                src_ref=cbuf.at[pl.ds(row, 256)], dst_ref=cbuf.at[pl.ds(1024 + row, 256)],
                send_sem=c_send.at[s], recv_sem=c_recv.at[s], device_id=partner, device_id_type=MESH,
            ).wait_recv()

        c = cbuf[pl.ds(pl.multiple_of(1024 * other + 256 * s, 256), 256), :]
        k = dot(c, wk_ref[...]).astype(BF)
        kc[0] = k[:, :128]
        kc[1] = k[:, 128:]
        v = dot_t(wvt[...], c).astype(BF)
        for h in range(HEADS):
            va[h, 0:32, :] = v[h * 32 : h * 32 + 32, :]
        held = (sa, sb)
        top = scores_of(0, sa)
        for h in range(HEADS):
            following = scores_of(h + 1, held[(h + 1) % 2]) if h + 1 < HEADS else None
            absorb(h, held[h % 2], top)
            top = following
        return carry

    lax.fori_loop(0, 8, coarse_block, 0)

    for load in loads[1:]:
        load.wait()
    turned_out = jnp.concatenate([acc[h, 0:32, :] / acc[h, 32:33, :] for h in range(HEADS)], axis=0)
    fm[...] = fm[...] + turned_out.T

    def finish(i, carry):
        rows = pl.ds(pl.multiple_of(i * 128, 128), 128)
        attended = fm[rows, :].astype(BF)
        residual = (tok_ref[rows, :].astype(F32) + dot(attended, wo_ref[...])).astype(BF)
        wide = residual.astype(F32)
        second = normalized(wide, gain2_ref[...])
        hidden = jax.nn.gelu(dot(second, up_ref[...]), approximate=True).astype(BF)
        out_ref[rows, :] = (wide + dot(hidden, down_ref[...])).astype(BF)
        return carry

    lax.fori_loop(0, 4, finish, 0)

    for copy in b_copies:
        copy.wait_send()
    for copy in c_copies:
        copy.wait_send()


def shards(
    tokens, norm_gain, query_weight, key_weight, value_weight, head_scale, out_weight, mlp_gain, up_weight, down_weight
):
    shape = tokens.shape
    vmem = pl.BlockSpec(memory_space=pltpu.VMEM)
    smem = pl.BlockSpec(memory_space=pltpu.SMEM)
    hbm = pl.BlockSpec(memory_space=pl.ANY)
    dma = pltpu.SemaphoreType.DMA
    V = pltpu.VMEM
    flat = pl.pallas_call(
        layer_kernel,
        out_shape=jax.ShapeDtypeStruct((512, 256), BF),
        in_specs=[vmem, vmem, vmem, vmem, vmem, smem, hbm, vmem, hbm, hbm, hbm, vmem],
        out_specs=vmem,
        scratch_shapes=[
            V((2, 512, 128), F32),
            V((2, 64, 128), F32),
            V((2, 128, 128), F32),
            V((2, 32, 128), F32),
            V((2, PACKED, 128), F32),
            V((PACKED, 256), BF),
            V((SRC, 256), BF),
            V((8, 8, 256), BF),
            V((2048, 256), BF),
            V((KEYS, 256), BF),
            V((512, 256), BF),
            V((8, 128, 512), BF),
            V((KEYS, 256), BF),
            V((KEYS, 256), BF),
            V((512, 256), F32),
            V((2, 256, 128), BF),
            V((8, 48, 256), BF),
            V((256, 512), F32),
            V((256, 512), F32),
            V((8, 512), F32),
            V((8, 48, 512), F32),
            V((256, 256), BF),
            V((256, 512), BF),
            V((512, 256), BF),
            V((KEYS - AT_Z, SRC), BF),
            V((256, 256), BF),
            dma((4,)),
            dma((26,)),
            dma((26,)),
            dma((8,)),
            dma((8,)),
            dma((4,)),
            dma((4,)),
            dma((4,)),
            dma((4,)),
            dma((4,)),
            dma((4,)),
        ],
        compiler_params=pltpu.CompilerParams(
            collective_id=0, has_side_effects=True, vmem_limit_bytes=60 << 20
        ),
        name="layer",
    )(
        tokens.reshape(512, 256),
        norm_gain.reshape(1, 256),
        query_weight,
        key_weight,
        value_weight,
        head_scale,
        out_weight,
        mlp_gain.reshape(1, 256),
        up_weight,
        down_weight,
        jnp.asarray(selection(), BF),
        jnp.asarray(window_mask()),
    )
    return flat.reshape(shape)


def solution(mesh):
    in_specs = (P("gx", "gy", "gz", None), P(), P(), P(), P(), P(), P(), P(), P(), P())
    step = jax.shard_map(shards, mesh=mesh, in_specs=in_specs, out_specs=P("gx", "gy", "gz", None), check_vma=False)

    def traced(*arguments):
        with jax.sharding.use_abstract_mesh(mesh.abstract_mesh):
            return step(*arguments)

    return traced
```

time: 642 us -> 50.4 us (0.08); the launches traced: 632 us -> 50.3 us
  waiting for transfers between devices: 424 us -> 0 us
  local copies, waits for them, and re-layouts: 74.8 us -> 1.67 us
  matrix products: 66.7 us -> 0 us
  Pallas kernels: 0 us -> 48.6 us
  other arithmetic: 27.4 us -> 0 us
  starting transfers between devices: 23.6 us -> 0 us
  between operations: 14.6 us -> 0.01 us
    all_gather x1 -> x0, waiting for transfers between devices: 424 us -> none  [shards(): portion = lax.all_gather(coarse, ('gx', 'gy', 'gz'), axis=0, tiled=True)]
    dot_general x21 -> x0, matrix products: 66.7 us -> none  [the longest x4 21.6 us: absorb(): jnp.einsum('qhd,khd->hqk', query_heads, key_heads, preferred_element_type...]
    pallas_call x0 -> x1, Pallas kernels: none -> 48.6 us  [shards(): pl.pallas_call(layer_kernel, out_shape=jax.ShapeDtypeStruct((512, 256), B...]
    another operation x12 -> x0, local copies, waits for them, and re-layouts: 24.2 us -> none  [the longest x2 11.8 us: window_attend(): key_cells = key_cells.reshape(windows, window_size, HEADS, head_width)]
    ppermute x12 -> x0, starting transfers between devices: 23.6 us -> none  [the longest x6 15.6 us: extended(): lax.ppermute(head, axis, [((i + 1) % count, i) for i in range(count)])]
    reduce_sum x11 -> x0, other arithmetic: 10.8 us -> none  [the longest x4 5.79 us: absorb(): summed = summed * shrink + jnp.sum(weights, axis=-1)]
    reshape x7 -> x0, local copies, waits for them, and re-layouts: 9.34 us -> none  [the longest x2 4.82 us: window_attend(): blended.reshape(along_x, along_y, along_z, query_side, query_side, query_...]
    slice x8 -> x0, local copies, waits for them, and re-layouts: 7.23 us -> none  [the longest x6 6.3 us: unfold_axis(): lower = lax.slice_in_dim(paired, 0, windows, axis=dimension)]
  transfers between devices with their start and end apart: 13 -> 0, of which waited for: 1 -> 0; matrix products, arithmetic and copies ran while one was open for 15% -> 0% of each run, Pallas kernels for 0% -> 0%
where the time goes in v1:
time: 50.4 us; the launch traced here: 50.3 us
  Pallas kernels  48.6 us (96%)
  local copies, waits for them, and re-layouts  1.67 us (3%)
    pallas_call x1, Pallas kernels, shards(): pl.pallas_call(layer_kernel, out_shape=jax.ShapeDtypeStruct((512, 256), B...  48.6 us
    unnamed x1, local copies, waits for them, and re-layouts  1.67 us

profile of v1, /device:TPU:1, one launch (start us, length us, event | category | flops | bytes accessed | tf_op | source)
XLA Modules:
  0.0 50.3 jit_solution(9491380631944470330)
XLA Ops:
  0.0 48.6 %layer.1 = bf16[512,256]{1,0:T(8,128)(2,1)} custom-call(bf16[512,256]{1,0:T(8,128)(2,1)} %bitcast.5, f32[1,256]{1,0:T(1,128)} %bitcast.6, bf16[256,256]{1,0:T(8,128)(2,1)} %wq_ref.1, bf16[256,256]{1,0:T(8,128)(2,1)} %wk_ref.1, bf16[256,256]{1,0:T(8,128)(2,1)} %wv_ref.1, f32[8]{0:T(128)} %scale_ref.1, bf16[256,256]{1,0:T(8,128)(2,1)} %wo_hbm.1, ...), custom_call_target="tpu_custom_call" | custom-call | tf_op jit(solution)/shard_map/layer/pallas_call | solution.py:441
  48.6 1.7 %copy.14 = bf16[8,8,8,256]{3,2,1,0:T(8,128)(2,1)} copy(bf16[8,8,8,256]{3,2,1,0:T(8,128)(2,1)} %bitcast.4) | data formatting | bytes 524288

commit v2 on v1

--- a/solution.py
+++ b/solution.py
@@ -16,6 +16,7 @@
 EPSILON = 1e-05
 LOG2E = math.log2(math.e)
 NEG = -1e30
+AHEAD = 3
 
 FACES = [(1, 0, 0), (-1, 0, 0), (0, 1, 0), (0, -1, 0), (0, 0, 1), (0, 0, -1)]
 OTHERS = [
@@ -77,20 +78,20 @@
     return pick
 
 
-def window_mask():
-    mask = np.full((8, 256), NEG, np.float32)
+def window_masks():
+    mask = np.full((8, 384), NEG, np.float32)
     for q in range(8):
         for lane in range(256):
             if lane < 128:
-                at, low = lane % 8 + 1, 2 * (q // 2)
+                at, low, put = lane % 8 + 1, 2 * (q // 2), lane
             elif lane < 160:
-                at, low = 9 * (lane % 2), 2 * (q // 2)
+                at, low, put = 9 * (lane % 2), 2 * (q // 2), lane
             elif lane < 224:
-                at, low = lane % 4 + 1, 2 * (q // 4)
+                at, low, put = lane % 4 + 1, 2 * (q // 4), lane + 128
             else:
-                at, low = 5 * (lane % 2), 2 * (q // 4)
+                at, low, put = 5 * (lane % 2), 2 * (q // 4), lane + 128
             if low <= at <= low + 3:
-                mask[q, lane] = 0
+                mask[q, put] = 0
     return mask
 
 
@@ -116,7 +117,7 @@
 def layer_kernel(
     tok_ref, gain_ref, wq_ref, wk_ref, wv_ref, scale_ref, wo_hbm, gain2_ref, up_hbm, down_hbm, pick_hbm, mask_ref,
     out_ref,
-    nf, mf, tf, cf, stage, packed, src, zbuf, cbuf, abuf, qn, qm, kbuf, vbuf, fm, kc, va, sa, sb, ms, acc,
+    nf, mf, tf, cf, stage, packed, src, zbuf, cbuf, abuf, qn, qm, kbuf, vbuf, wbuf, fm, kc, va, held, ms, acc,
     wo_ref, up_ref, down_ref, pick_ref, wvt,
     load_sem, halo_send, halo_recv, z_send, z_recv, a_send, a_recv, b_send, b_recv, c_send, c_recv,
 ):
@@ -134,11 +135,11 @@
     ]
     along_z = [(gx, gy, lax.rem(gz + k, 8)) for k in range(1, 8)]
     first = [chip(lax.rem(xpos + k * (1 - core), 4), lax.rem(ypos + k * core, 4)) for k in range(1, 4)]
-    then = [chip(lax.rem(xpos + k * core, 4), lax.rem(ypos + k * (1 - core), 4)) for k in range(1, 4)]
+    then = [chip(lax.rem(xpos + k * core, 4), lax.rem(ypos + k * (1 - core), 4)) for k in (1, 3)]
     partner = (gx + 1 - 2 * core, gy, gz)
 
     barrier = pltpu.get_barrier_semaphore()
-    greeted = near + along_z + first + then
+    greeted = near + along_z[1:6] + first + then
     for peer in greeted:
         pl.semaphore_signal(barrier, inc=1, device_id=peer, device_id_type=MESH)
 
@@ -209,7 +210,7 @@
 
     z_copies = [
         pltpu.make_async_remote_copy(
-            src_ref=zbuf.at[0], dst_ref=zbuf.at[k], send_sem=z_send.at[k], recv_sem=z_recv.at[k],
+            src_ref=zbuf.at[0], dst_ref=zbuf.at[k], send_sem=z_send, recv_sem=z_recv,
             device_id=along_z[k - 1], device_id_type=MESH,
         )
         for k in range(1, 8)
@@ -223,7 +224,7 @@
         halo.append(
             pltpu.make_async_remote_copy(
                 src_ref=packed.at[pl.ds(start, rows)], dst_ref=src.at[pl.ds(land, rows)],
-                send_sem=halo_send.at[i], recv_sem=halo_recv.at[i], device_id=near[i], device_id_type=MESH,
+                send_sem=halo_send, recv_sem=halo_recv, device_id=near[i], device_id_type=MESH,
             )
         )
     for copy in halo:
@@ -245,21 +246,25 @@
     ms[...] = jnp.full_like(ms, NEG)
     acc[...] = jnp.zeros_like(acc)
 
-    for copy in z_copies:
-        copy.wait()
+    pltpu.make_async_remote_copy(
+        src_ref=zbuf.at[pl.ds(1, 7)], dst_ref=zbuf.at[pl.ds(1, 7)], send_sem=z_send, recv_sem=z_recv,
+        device_id=along_z[0], device_id_type=MESH,
+    ).wait()
     cbuf[0:64, :] = zbuf[...].astype(F32).reshape(64, 256).astype(BF)
     a_copies = [
         pltpu.make_async_remote_copy(
             src_ref=cbuf.at[pl.ds(0, 64)], dst_ref=cbuf.at[pl.ds(64 * k, 64)],
-            send_sem=a_send.at[k], recv_sem=a_recv.at[k], device_id=first[k - 1], device_id_type=MESH,
+            send_sem=a_send, recv_sem=a_recv, device_id=first[k - 1], device_id_type=MESH,
         )
         for k in range(1, 4)
     ]
     for copy in a_copies:
         copy.start()
 
-    for copy in halo:
-        copy.wait()
+    pltpu.make_async_remote_copy(
+        src_ref=packed, dst_ref=packed, send_sem=halo_send, recv_sem=halo_recv,
+        device_id=near[0], device_id_type=MESH,
+    ).wait()
 
     def cells(d, row):
         start, _ = slot(d)
@@ -282,112 +287,132 @@
     loads[0].wait()
     abuf[AT_Z:KEYS, :] = dot(pick_ref[...], src[...]).astype(BF)
 
-    def project(i, carry):
-        rows = pl.ds(pl.multiple_of(i * 128, 128), 128)
+    pltpu.make_async_remote_copy(
+        src_ref=cbuf.at[pl.ds(64, 192)], dst_ref=cbuf.at[pl.ds(64, 192)], send_sem=a_send, recv_sem=a_recv,
+        device_id=first[0], device_id_type=MESH,
+    ).wait()
+
+    def ring(start, land, count, k, peer):
+        return pltpu.make_async_remote_copy(
+            src_ref=cbuf.at[pl.ds(start, count)], dst_ref=cbuf.at[pl.ds(land, count)],
+            send_sem=b_send, recv_sem=b_recv.at[k], device_id=peer, device_id_type=MESH,
+        )
+
+    def block(k):
+        return pl.ds(k * 256 if isinstance(k, int) else pl.multiple_of(k * 256, 256), 256)
+
+    def swap(k):
+        return pltpu.make_async_remote_copy(
+            src_ref=cbuf.at[block(k)], dst_ref=cbuf.at[block(k + 4)],
+            send_sem=c_send, recv_sem=c_recv.at[k], device_id=partner, device_id_type=MESH,
+        )
+
+    ring(0, 256, 256, 1, then[0]).start()
+    ring(0, 512, 256, 2, then[1]).start()
+    swap(0).start()
+
+    for i in range(4):
+        rows = slice(i * 352, i * 352 + 352)
         a = abuf[rows, :]
         kbuf[rows, :] = dot(a, wk_ref[...]).astype(BF)
         vbuf[rows, :] = dot(a, wv_ref[...]).astype(BF)
-        return carry
-
-    lax.fori_loop(0, KEYS // 128, project, 0)
-
-    for copy in a_copies:
-        copy.wait()
-    b_copies = [
-        pltpu.make_async_remote_copy(
-            src_ref=cbuf.at[pl.ds(0, 256)], dst_ref=cbuf.at[pl.ds(256 * k, 256)],
-            send_sem=b_send.at[k], recv_sem=b_recv.at[k], device_id=then[k - 1], device_id_type=MESH,
-        )
-        for k in range(1, 4)
-    ]
-    for copy in b_copies:
-        copy.start()
-    c_copies = [
-        pltpu.make_async_remote_copy(
-            src_ref=cbuf.at[pl.ds(256 * k, 256)], dst_ref=cbuf.at[pl.ds(1024 + 256 * k, 256)],
-            send_sem=c_send.at[k], recv_sem=c_recv.at[k], device_id=partner, device_id_type=MESH,
-        )
-        for k in range(4)
-    ]
-    c_copies[0].start()
-
-    lane = lax.broadcasted_iota(jnp.int32, (1, 128), 1)
-    is_fine = lane < 32
-
-    def windows(g, carry):
-        bx, by = lax.div(g, 4), lax.rem(g, 4)
-        mx, my = lax.div(bx, 2), lax.div(by, 2)
+
+    lane_quad = lax.broadcasted_iota(jnp.int32, (1, 128), 1) // 32
+    blank_f, blank_m = jnp.zeros((160, 128), BF), jnp.zeros((96, 128), BF)
+    tally = jnp.concatenate(
+        [
+            jnp.concatenate([jnp.ones((160, 128), BF), blank_m], axis=0),
+            jnp.concatenate([blank_f, jnp.ones((96, 128), BF)], axis=0),
+        ],
+        axis=1,
+    )
+
+    def windows(bx, carry):
+        mx = lax.div(bx, 2)
 
         def rows(start, count):
             return pl.ds(pl.multiple_of(start, 16), count)
 
-        r0 = rows(bx * 128 + by * 16, 16)
-        r1 = rows(bx * 128 + by * 16 + 64, 16)
-        parts = [rows((2 * bx + i) * 80 + by * 16, 32) for i in range(4)] + [
-            rows(AT_Z + by * 80 + bx * 16, 32),
-            rows(AT_M + my * 96 + mx * 32, 64),
-            rows(AT_MZ + my * 48 + mx * 16, 32),
-        ]
-        q = jnp.concatenate([qn[r0, :], qn[r1, :]], axis=0)
-        spread_q = jnp.concatenate(
-            [jnp.where(lane_head == h, q, jnp.zeros_like(q)) for h in range(HEADS)], axis=0
-        )
-        keys = jnp.concatenate([kbuf[p, :] for p in parts], axis=0)
-        values = jnp.concatenate([vbuf[p, :] for p in parts], axis=0)
-        scores = (dot_t(spread_q, keys).reshape(32, 8, 256) + mask_ref[...][None]).reshape(256, 256)
-        s0, s1 = scores[:, :128], scores[:, 128:]
-        top_f = jnp.max(jnp.maximum(s0, jnp.where(is_fine, s1, NEG)), axis=1, keepdims=True)
-        top_m = jnp.max(jnp.where(is_fine, NEG, s1), axis=1, keepdims=True)
-        e0 = jnp.exp2(s0 - top_f)
-        e1 = jnp.exp2(s1 - jnp.where(is_fine, top_f, top_m))
-        sum_f = jnp.sum(e0 + jnp.where(is_fine, e1, 0.0), axis=1, keepdims=True)
-        sum_m = jnp.sum(jnp.where(is_fine, 0.0, e1), axis=1, keepdims=True)
-        inv_f, inv_m = 1.0 / sum_f, 1.0 / sum_m
-        weights = jnp.concatenate([e0 * inv_f, e1 * jnp.where(is_fine, inv_f, inv_m)], axis=1).astype(BF)
-        mixed = dot(weights, values)
-        total = jnp.zeros((32, 256), F32)
-        for h in range(HEADS):
-            total = jnp.where(lane_head == h, mixed[h * 32 : h * 32 + 32, :], total)
-        fm[r0, :] = total[:16]
-        fm[r1, :] = total[16:]
+        def places(by):
+            my = by // 2
+            parts = [rows((2 * bx + i) * 80 + by * 16, 32) for i in range(4)] + [
+                rows(AT_Z + by * 80 + bx * 16, 32),
+                rows(AT_M + my * 96 + mx * 32, 64),
+                rows(AT_MZ + my * 48 + mx * 16, 32),
+            ]
+            return rows(bx * 128 + by * 16, 16), rows(bx * 128 + by * 16 + 64, 16), parts
+
+        def begin(unit):
+            r0, r1, parts = places(unit // 2)
+            lanes = slice(unit % 2 * 128, unit % 2 * 128 + 128)
+            q = jnp.concatenate([qn[r0, lanes], qn[r1, lanes]], axis=0)
+            heads = jnp.concatenate([jnp.where(lane_quad == h, q, jnp.zeros_like(q)) for h in range(4)], axis=0)
+            keys = jnp.concatenate([kbuf[p, lanes] for p in parts], axis=0)
+            wbuf[unit] = dot_t(heads, keys)
+
+        def end(unit):
+            r0, r1, parts = places(unit // 2)
+            lanes = slice(unit % 2 * 128, unit % 2 * 128 + 128)
+            fine = jnp.concatenate([vbuf[p, lanes] for p in parts[:5]] + [blank_m], axis=0)
+            mids = jnp.concatenate([blank_f] + [vbuf[p, lanes] for p in parts[5:]], axis=0)
+            left = wbuf[unit, :, 0:128].reshape(16, 8, 128)
+            right = wbuf[unit, :, 128:256].reshape(16, 8, 128)
+            s0 = (left + mask_ref[:, 0:128][None]).reshape(128, 128)
+            sf = (right + mask_ref[:, 128:256][None]).reshape(128, 128)
+            sm = (right + mask_ref[:, 256:384][None]).reshape(128, 128)
+            top_f = jnp.max(jnp.maximum(s0, sf), axis=1, keepdims=True)
+            top_m = jnp.max(sm, axis=1, keepdims=True)
+            e = jnp.concatenate(
+                [jnp.exp2(s0 - top_f), jnp.exp2(jnp.maximum(sf - top_f, sm - top_m))], axis=1
+            ).astype(BF)
+            mixed = dot(e, jnp.concatenate([fine, mids], axis=1)) / dot(e, tally)
+            mixed = mixed[:, :128] + mixed[:, 128:]
+            total = mixed[0:32, :]
+            for h in range(1, 4):
+                total = jnp.where(lane_quad == h, mixed[h * 32 : h * 32 + 32, :], total)
+            fm[r0, lanes] = total[:16]
+            fm[r1, lanes] = total[16:]
+
+        for unit in range(AHEAD):
+            begin(unit)
+        for unit in range(8):
+            if unit + AHEAD < 8:
+                begin(unit + AHEAD)
+            end(unit)
         return carry
 
-    lax.fori_loop(0, 16, windows, 0)
-
-    def scores_of(h, into):
+    lax.fori_loop(0, 4, windows, 0)
+
+    ring(256, 256, 256, 1, then[0]).wait_recv()
+    ring(256, 768, 128, 3, then[0]).start()
+    ring(512, 512, 256, 2, then[1]).wait_recv()
+    ring(640, 896, 128, 3, then[1]).start()
+    swap(1).start()
+    swap(2).start()
+
+    def scores_of(h):
         s = dot(kc[h // 4], qm[h])
-        into[...] = s
-        return jnp.max(s, axis=0, keepdims=True)
-
-    def absorb(h, held, block_top):
-        old = ms[h : h + 1, :]
-        top = jnp.maximum(old, block_top)
-        p = jnp.exp2(held[...] - top).astype(BF)
+        held[h] = s
+        return jnp.max(s.reshape(32, 8, 512), axis=0)
+
+    def absorb(h, block_top):
+        old = ms[h]
+        top = jnp.maximum(old, jnp.max(block_top, axis=0, keepdims=True))
+        p = jnp.exp2(held[h] - top).astype(BF)
         acc[h] = acc[h] * jnp.exp2(old - top) + dot(va[h], p)
-        ms[h : h + 1, :] = top
+        ms[h] = top
 
     def coarse_block(j, carry):
         s, other = lax.div(j, 2), lax.rem(j, 2)
 
-        @pl.when(jnp.logical_and(other == 0, s > 0))
+        @pl.when(j == 3)
         def _():
-            row = pl.multiple_of(256 * s, 256)
-            pltpu.make_async_remote_copy(
-                src_ref=cbuf.at[pl.ds(0, 256)], dst_ref=cbuf.at[pl.ds(row, 256)],
-                send_sem=b_send.at[s], recv_sem=b_recv.at[s], device_id=then[0], device_id_type=MESH,
-            ).wait_recv()
-            pltpu.make_async_remote_copy(
-                src_ref=cbuf.at[pl.ds(row, 256)], dst_ref=cbuf.at[pl.ds(1024 + row, 256)],
-                send_sem=c_send.at[s], recv_sem=c_recv.at[s], device_id=partner, device_id_type=MESH,
-            ).start()
+            ring(768, 768, 256, 3, then[0]).wait_recv()
+            swap(3).start()
 
         @pl.when(other == 1)
         def _():
-            row = pl.multiple_of(256 * s, 256)
-            pltpu.make_async_remote_copy(
-                src_ref=cbuf.at[pl.ds(row, 256)], dst_ref=cbuf.at[pl.ds(1024 + row, 256)],
-                send_sem=c_send.at[s], recv_sem=c_recv.at[s], device_id=partner, device_id_type=MESH,
-            ).wait_recv()
+            swap(s).wait_recv()
 
         c = cbuf[pl.ds(pl.multiple_of(1024 * other + 256 * s, 256), 256), :]
         k = dot(c, wk_ref[...]).astype(BF)
@@ -396,12 +421,11 @@
         v = dot_t(wvt[...], c).astype(BF)
         for h in range(HEADS):
             va[h, 0:32, :] = v[h * 32 : h * 32 + 32, :]
-        held = (sa, sb)
-        top = scores_of(0, sa)
+        tops = [scores_of(h) for h in range(3)]
         for h in range(HEADS):
-            following = scores_of(h + 1, held[(h + 1) % 2]) if h + 1 < HEADS else None
-            absorb(h, held[h % 2], top)
-            top = following
+            if h + 3 < HEADS:
+                tops.append(scores_of(h + 3))
+            absorb(h, tops[h])
         return carry
 
     lax.fori_loop(0, 8, coarse_block, 0)
@@ -411,22 +435,23 @@
     turned_out = jnp.concatenate([acc[h, 0:32, :] / acc[h, 32:33, :] for h in range(HEADS)], axis=0)
     fm[...] = fm[...] + turned_out.T
 
-    def finish(i, carry):
-        rows = pl.ds(pl.multiple_of(i * 128, 128), 128)
+    for i in range(4):
+        rows = slice(i * 128, i * 128 + 128)
         attended = fm[rows, :].astype(BF)
         residual = (tok_ref[rows, :].astype(F32) + dot(attended, wo_ref[...])).astype(BF)
         wide = residual.astype(F32)
         second = normalized(wide, gain2_ref[...])
         hidden = jax.nn.gelu(dot(second, up_ref[...]), approximate=True).astype(BF)
         out_ref[rows, :] = (wide + dot(hidden, down_ref[...])).astype(BF)
-        return carry
-
-    lax.fori_loop(0, 4, finish, 0)
-
-    for copy in b_copies:
-        copy.wait_send()
-    for copy in c_copies:
-        copy.wait_send()
+
+    pltpu.make_async_remote_copy(
+        src_ref=cbuf.at[pl.ds(256, 768)], dst_ref=cbuf.at[pl.ds(256, 768)], send_sem=b_send, recv_sem=b_recv.at[0],
+        device_id=then[0], device_id_type=MESH,
+    ).wait_send()
+    pltpu.make_async_remote_copy(
+        src_ref=cbuf.at[pl.ds(0, 1024)], dst_ref=cbuf.at[pl.ds(0, 1024)], send_sem=c_send, recv_sem=c_recv.at[0],
+        device_id=partner, device_id_type=MESH,
+    ).wait_send()
 
 
 def shards(
@@ -458,12 +483,12 @@
             V((8, 128, 512), BF),
             V((KEYS, 256), BF),
             V((KEYS, 256), BF),
+            V((8, 128, 256), F32),
             V((512, 256), F32),
             V((2, 256, 128), BF),
             V((8, 48, 256), BF),
-            V((256, 512), F32),
-            V((256, 512), F32),
-            V((8, 512), F32),
+            V((8, 256, 512), F32),
+            V((8, 1, 512), F32),
             V((8, 48, 512), F32),
             V((256, 256), BF),
             V((256, 512), BF),
@@ -471,15 +496,15 @@
             V((KEYS - AT_Z, SRC), BF),
             V((256, 256), BF),
             dma((4,)),
-            dma((26,)),
-            dma((26,)),
-            dma((8,)),
-            dma((8,)),
+            dma,
+            dma,
+            dma,
+            dma,
+            dma,
+            dma,
+            dma,
             dma((4,)),
-            dma((4,)),
-            dma((4,)),
-            dma((4,)),
-            dma((4,)),
+            dma,
             dma((4,)),
         ],
         compiler_params=pltpu.CompilerParams(
@@ -498,7 +523,7 @@
         up_weight,
         down_weight,
         jnp.asarray(selection(), BF),
-        jnp.asarray(window_mask()),
+        jnp.asarray(window_masks()),
     )
     return flat.reshape(shape)
 

time: 50.4 us -> 39.9 us (0.79)
  Pallas kernels: 48.6 us -> 38.1 us
    pallas_call x1, Pallas kernels: 48.6 us -> 38.1 us  [shards(): pl.pallas_call(layer_kernel, out_shape=jax.ShapeDtypeStruct((512, 256), B...]
where the time goes in v2:
time: 39.9 us; the launch traced here: 39.8 us
  Pallas kernels  38.1 us (95%)
  local copies, waits for them, and re-layouts  1.67 us (4%)
    pallas_call x1, Pallas kernels, shards(): pl.pallas_call(layer_kernel, out_shape=jax.ShapeDtypeStruct((512, 256), B...  38.1 us
    unnamed x1, local copies, waits for them, and re-layouts  1.67 us

profile of v2, /device:TPU:1, one launch (start us, length us, event | category | flops | bytes accessed | tf_op | source)
XLA Modules:
  0.0 39.8 jit_solution(3764187880310723247)
XLA Ops:
  0.0 38.1 %layer.1 = bf16[512,256]{1,0:T(8,128)(2,1)} custom-call(bf16[512,256]{1,0:T(8,128)(2,1)} %bitcast.5, f32[1,256]{1,0:T(1,128)} %bitcast.6, bf16[256,256]{1,0:T(8,128)(2,1)} %wq_ref.1, bf16[256,256]{1,0:T(8,128)(2,1)} %wk_ref.1, bf16[256,256]{1,0:T(8,128)(2,1)} %wv_ref.1, f32[8]{0:T(128)} %scale_ref.1, bf16[256,256]{1,0:T(8,128)(2,1)} %wo_hbm.1, ...), custom_call_target="tpu_custom_call" | custom-call | tf_op jit(solution)/shard_map/layer/pallas_call | solution.py:466
  38.1 1.7 %copy.14 = bf16[8,8,8,256]{3,2,1,0:T(8,128)(2,1)} copy(bf16[8,8,8,256]{3,2,1,0:T(8,128)(2,1)} %bitcast.4) | data formatting | bytes 524288

commit v3 on v2

--- a/solution.py
+++ b/solution.py
@@ -115,12 +115,24 @@
 
 
 def layer_kernel(
-    tok_ref, gain_ref, wq_ref, wk_ref, wv_ref, scale_ref, wo_hbm, gain2_ref, up_hbm, down_hbm, pick_hbm, mask_ref,
+    tok_hbm, gain_hbm, wq_hbm, wk_hbm, wv_hbm, scale_hbm, pick_hbm, mask_hbm,
     out_ref,
     nf, mf, tf, cf, stage, packed, src, zbuf, cbuf, abuf, qn, qm, kbuf, vbuf, wbuf, fm, kc, va, held, ms, acc,
-    wo_ref, up_ref, down_ref, pick_ref, wvt,
+    tok_ref, gain_ref, wq_ref, wk_ref, wv_ref, scale_ref, pick_ref, mask_ref, wvt,
     load_sem, halo_send, halo_recv, z_send, z_recv, a_send, a_recv, b_send, b_recv, c_send, c_recv,
 ):
+    loads = [
+        pltpu.make_async_copy(a, b, load_sem.at[i])
+        for i, (a, b) in enumerate(
+            (
+                (tok_hbm, tok_ref), (gain_hbm, gain_ref), (scale_hbm, scale_ref), (wq_hbm, wq_ref), (wv_hbm, wv_ref),
+                (wk_hbm, wk_ref), (pick_hbm, pick_ref), (mask_hbm, mask_ref),
+            )
+        )
+    ]
+    for load in loads:
+        load.start()
+
     gx, gy, gz = lax.axis_index("gx"), lax.axis_index("gy"), lax.axis_index("gz")
     core, ylow = lax.rem(gx, 2), lax.div(gx, 2)
     xpos, yhigh = lax.div(gy, 2), lax.rem(gy, 2)
@@ -139,19 +151,12 @@
     partner = (gx + 1 - 2 * core, gy, gz)
 
     barrier = pltpu.get_barrier_semaphore()
-    greeted = near + along_z[1:6] + first + then
+    greeted = along_z[1:6] + near[::-1] + first + then
     for peer in greeted:
         pl.semaphore_signal(barrier, inc=1, device_id=peer, device_id_type=MESH)
 
-    loads = [
-        pltpu.make_async_copy(a, b, load_sem.at[i])
-        for i, (a, b) in enumerate(
-            ((pick_hbm, pick_ref), (wo_hbm, wo_ref), (up_hbm, up_ref), (down_hbm, down_ref))
-        )
-    ]
-    for load in loads:
-        load.start()
-
+    loads[0].wait()
+    loads[1].wait()
     normed = normalized(tok_ref[...].astype(F32), gain_ref[...])
     widened = normed.astype(F32)
     for c in range(2):
@@ -230,6 +235,8 @@
     for copy in halo:
         copy.start()
 
+    for load in loads[2:5]:
+        load.wait()
     factor = LOG2E / math.sqrt(32)
     lane_head = lax.broadcasted_iota(jnp.int32, (1, 256), 1) // 32
     spread = jnp.zeros((1, 256), F32)
@@ -242,7 +249,8 @@
         at = (h % 4) * 32
         qm[h, at : at + 32, :] = (turned[h * 32 : h * 32 + 32, :] * (scale_ref[h] * factor)).astype(BF)
     wvt[...] = wv_ref[...].T
-    va[:, 32:48, :] = jnp.ones((HEADS, 16, 256), BF)
+    for part in range(2):
+        va[part, :, 32:48, :] = jnp.ones((HEADS, 16, 256), BF)
     ms[...] = jnp.full_like(ms, NEG)
     acc[...] = jnp.zeros_like(acc)
 
@@ -284,7 +292,8 @@
             own = slice((x - 1) * 64, x * 64)
             inner = jnp.concatenate([nf[0, own, :], nf[1, own, :]], axis=1)
         abuf[x * 80 : x * 80 + 80, :] = jnp.concatenate([begin, inner, end], axis=0).astype(BF)
-    loads[0].wait()
+    for load in loads[5:]:
+        load.wait()
     abuf[AT_Z:KEYS, :] = dot(pick_ref[...], src[...]).astype(BF)
 
     pltpu.make_async_remote_copy(
@@ -390,59 +399,55 @@
     swap(1).start()
     swap(2).start()
 
-    def scores_of(h):
-        s = dot(kc[h // 4], qm[h])
-        held[h] = s
+    def scores_of(unit):
+        part, h = unit // HEADS, unit % HEADS
+        s = dot(kc[part, h // 4], qm[h])
+        held[unit] = s
         return jnp.max(s.reshape(32, 8, 512), axis=0)
 
-    def absorb(h, block_top):
+    def absorb(unit, block_top):
+        part, h = unit // HEADS, unit % HEADS
         old = ms[h]
         top = jnp.maximum(old, jnp.max(block_top, axis=0, keepdims=True))
-        p = jnp.exp2(held[h] - top).astype(BF)
-        acc[h] = acc[h] * jnp.exp2(old - top) + dot(va[h], p)
+        p = jnp.exp2(held[unit] - top).astype(BF)
+        acc[h] = acc[h] * jnp.exp2(old - top) + dot(va[part, h], p)
         ms[h] = top
 
     def coarse_block(j, carry):
-        s, other = lax.div(j, 2), lax.rem(j, 2)
-
-        @pl.when(j == 3)
+        @pl.when(j == 1)
         def _():
             ring(768, 768, 256, 3, then[0]).wait_recv()
             swap(3).start()
 
-        @pl.when(other == 1)
-        def _():
-            swap(s).wait_recv()
-
-        c = cbuf[pl.ds(pl.multiple_of(1024 * other + 256 * s, 256), 256), :]
-        k = dot(c, wk_ref[...]).astype(BF)
-        kc[0] = k[:, :128]
-        kc[1] = k[:, 128:]
-        v = dot_t(wvt[...], c).astype(BF)
-        for h in range(HEADS):
-            va[h, 0:32, :] = v[h * 32 : h * 32 + 32, :]
+        swap(j).wait_recv()
+
+        def project_keys(part):
+            k = dot(cbuf[block(j + 4 * part), :], wk_ref[...]).astype(BF)
+            kc[part, 0] = k[:, :128]
+            kc[part, 1] = k[:, 128:]
+
+        def project_values(part):
+            v = dot_t(wvt[...], cbuf[block(j + 4 * part), :]).astype(BF)
+            for h in range(HEADS):
+                va[part, h, 0:32, :] = v[h * 32 : h * 32 + 32, :]
+
+        project_keys(0)
         tops = [scores_of(h) for h in range(3)]
-        for h in range(HEADS):
-            if h + 3 < HEADS:
-                tops.append(scores_of(h + 3))
-            absorb(h, tops[h])
+        project_values(0)
+        for unit in range(2 * HEADS):
+            if unit == 2:
+                project_keys(1)
+            if unit == 4:
+                project_values(1)
+            if unit + 3 < 2 * HEADS:
+                tops.append(scores_of(unit + 3))
+            absorb(unit, tops[unit])
         return carry
 
-    lax.fori_loop(0, 8, coarse_block, 0)
-
-    for load in loads[1:]:
-        load.wait()
+    lax.fori_loop(0, 4, coarse_block, 0)
+
     turned_out = jnp.concatenate([acc[h, 0:32, :] / acc[h, 32:33, :] for h in range(HEADS)], axis=0)
-    fm[...] = fm[...] + turned_out.T
-
-    for i in range(4):
-        rows = slice(i * 128, i * 128 + 128)
-        attended = fm[rows, :].astype(BF)
-        residual = (tok_ref[rows, :].astype(F32) + dot(attended, wo_ref[...])).astype(BF)
-        wide = residual.astype(F32)
-        second = normalized(wide, gain2_ref[...])
-        hidden = jax.nn.gelu(dot(second, up_ref[...]), approximate=True).astype(BF)
-        out_ref[rows, :] = (wide + dot(hidden, down_ref[...])).astype(BF)
+    out_ref[...] = (fm[...] + turned_out.T).astype(BF)
 
     pltpu.make_async_remote_copy(
         src_ref=cbuf.at[pl.ds(256, 768)], dst_ref=cbuf.at[pl.ds(256, 768)], send_sem=b_send, recv_sem=b_recv.at[0],
@@ -454,19 +459,29 @@
     ).wait_send()
 
 
+def finish_kernel(att_ref, tok_ref, wo_ref, gain2_ref, up_ref, down_ref, out_ref):
+    for i in range(4):
+        rows = slice(i * 128, i * 128 + 128)
+        residual = (tok_ref[rows, :].astype(F32) + dot(att_ref[rows, :], wo_ref[...])).astype(BF)
+        wide = residual.astype(F32)
+        second = normalized(wide, gain2_ref[...])
+        hidden = jax.nn.gelu(dot(second, up_ref[...]), approximate=True).astype(BF)
+        out_ref[rows, :] = (wide + dot(hidden, down_ref[...])).astype(BF)
+
+
 def shards(
     tokens, norm_gain, query_weight, key_weight, value_weight, head_scale, out_weight, mlp_gain, up_weight, down_weight
 ):
     shape = tokens.shape
     vmem = pl.BlockSpec(memory_space=pltpu.VMEM)
-    smem = pl.BlockSpec(memory_space=pltpu.SMEM)
-    hbm = pl.BlockSpec(memory_space=pl.ANY)
+    hbm = pl.BlockSpec(memory_space=pltpu.MemorySpace.HBM)
     dma = pltpu.SemaphoreType.DMA
     V = pltpu.VMEM
-    flat = pl.pallas_call(
+    flat_tokens = tokens.reshape(512, 256)
+    attended = pl.pallas_call(
         layer_kernel,
         out_shape=jax.ShapeDtypeStruct((512, 256), BF),
-        in_specs=[vmem, vmem, vmem, vmem, vmem, smem, hbm, vmem, hbm, hbm, hbm, vmem],
+        in_specs=[hbm] * 8,
         out_specs=vmem,
         scratch_shapes=[
             V((2, 512, 128), F32),
@@ -485,17 +500,21 @@
             V((KEYS, 256), BF),
             V((8, 128, 256), F32),
             V((512, 256), F32),
-            V((2, 256, 128), BF),
-            V((8, 48, 256), BF),
-            V((8, 256, 512), F32),
+            V((2, 2, 256, 128), BF),
+            V((2, 8, 48, 256), BF),
+            V((16, 256, 512), F32),
             V((8, 1, 512), F32),
             V((8, 48, 512), F32),
+            V((512, 256), BF),
+            V((1, 256), F32),
             V((256, 256), BF),
-            V((256, 512), BF),
-            V((512, 256), BF),
+            V((256, 256), BF),
+            V((256, 256), BF),
+            pltpu.SMEM((8,), F32),
             V((KEYS - AT_Z, SRC), BF),
+            V((8, 384), F32),
             V((256, 256), BF),
-            dma((4,)),
+            dma((8,)),
             dma,
             dma,
             dma,
@@ -508,23 +527,32 @@
             dma((4,)),
         ],
         compiler_params=pltpu.CompilerParams(
-            collective_id=0, has_side_effects=True, vmem_limit_bytes=60 << 20
+            collective_id=0, has_side_effects=True, vmem_limit_bytes=28 << 20
         ),
         name="layer",
     )(
-        tokens.reshape(512, 256),
-        norm_gain.reshape(1, 256),
-        query_weight,
-        key_weight,
-        value_weight,
-        head_scale,
-        out_weight,
-        mlp_gain.reshape(1, 256),
-        up_weight,
-        down_weight,
-        jnp.asarray(selection(), BF),
-        jnp.asarray(window_masks()),
+        *(
+            pltpu.with_memory_space_constraint(a, pltpu.MemorySpace.HBM)
+            for a in (
+                flat_tokens,
+                norm_gain.reshape(1, 256),
+                query_weight,
+                key_weight,
+                value_weight,
+                head_scale,
+                jnp.asarray(selection(), BF),
+                jnp.asarray(window_masks()),
+            )
+        )
     )
+    flat = pl.pallas_call(
+        finish_kernel,
+        out_shape=jax.ShapeDtypeStruct((512, 256), BF),
+        in_specs=[vmem] * 6,
+        out_specs=vmem,
+        compiler_params=pltpu.CompilerParams(vmem_limit_bytes=12 << 20),
+        name="finish",
+    )(attended, flat_tokens, out_weight, mlp_gain.reshape(1, 256), up_weight, down_weight)
     return flat.reshape(shape)
 
 

time: 39.9 us -> 37.3 us (0.935)
  local copies, waits for them, and re-layouts: 1.67 us -> 0.02 us
  Pallas kernels: 38.1 us -> 37.1 us
    pallas_call x1, Pallas kernels: 38.1 us -> 34.6 us  [shards(): pl.pallas_call(layer_kernel, out_shape=jax.ShapeDtypeStruct((512, 256), B...]
    pallas_call x0 -> x1, Pallas kernels: none -> 2.53 us  [shards(): pl.pallas_call(finish_kernel, out_shape=jax.ShapeDtypeStruct((512, 256),...]
    unnamed x1 -> x10, local copies, waits for them, and re-layouts: 1.67 us -> 0.02 us
where the time goes in v3:
time: 37.3 us; the launch traced here: 37.2 us
  Pallas kernels  37.1 us (99%)
    pallas_call x1, Pallas kernels, shards(): pl.pallas_call(layer_kernel, out_shape=jax.ShapeDtypeStruct((512, 256), B...  34.6 us
    pallas_call x1, Pallas kernels, shards(): pl.pallas_call(finish_kernel, out_shape=jax.ShapeDtypeStruct((512, 256),...  2.53 us

profile of v3, /device:TPU:1, one launch (start us, length us, event | category | flops | bytes accessed | tf_op | source)
XLA Modules:
  0.0 37.2 jit_solution(15018864341027378384)
XLA Ops:
  0.0 0.0 copy-start.2
  0.0 0.0 copy-start.1
  0.0 0.0 copy-start.4
  0.0 0.0 copy-start.3
  0.0 0.0 copy-start
  0.0 34.6 %layer.1.att_ref = bf16[512,256]{1,0:T(8,128)(2,1)S(1)} custom-call(bf16[512,256]{1,0:T(8,128)(2,1)} %bitcast.4, f32[1,256]{1,0:T(1,128)} %bitcast.7, bf16[256,256]{1,0:T(8,128)(2,1)} %wq_hbm.1, bf16[256,256]{1,0:T(8,128)(2,1)} %wk_hbm.1, bf16[256,256]{1,0:T(8,128)(2,1)} %wv_hbm.1, f32[8]{0:T(128)} %scale_hbm.1, bf16[608,1024]{1,0:T(8,128)(2,1)} %constant.4.clone.pick_hbm, ...), custom_call_target="tpu_custom_call" | custom-call | tf_op jit(solution)/shard_map/layer/pallas_call | solution.py:481
  34.6 0.0 copy-done.2
  34.7 0.0 copy-done.1
  34.7 0.0 copy-done.4
  34.7 0.0 copy-done.3
  34.7 0.0 copy-done
  34.7 2.5 %finish.1 = bf16[512,256]{1,0:T(8,128)(2,1)} custom-call(bf16[512,256]{1,0:T(8,128)(2,1)S(1)} %layer.1.att_ref, bf16[512,256]{1,0:T(8,128)(2,1)S(1)} %bitcast.5, bf16[256,256]{1,0:T(8,128)(2,1)S(1)} %copy-done.3, f32[1,256]{1,0:T(1,128)S(1)} %bitcast.6, bf16[256,512]{1,0:T(8,128)(2,1)S(1)} %copy-done.1, bf16[512,256]{1,0:T(8,128)(2,1)S(1)} %copy-done.2), custom_call_target="tpu_custom_call" | custom-call | tf_op jit(solution)/shard_map/finish/pallas_call | solution.py:548
Async XLA Ops:
  0.0 34.6 %copy-start.2 = (bf16[512,256]{1,0:T(8,128)(2,1)S(1)}, bf16[512,256]{1,0:T(8,128)(2,1)}, u32[]{:S(2)}) copy-start(bf16[512,256]{1,0:T(8,128)(2,1)} %down_ref.1) | copy-start | bytes 786436
  0.0 34.7 %copy-start.1 = (bf16[256,512]{1,0:T(8,128)(2,1)S(1)}, bf16[256,512]{1,0:T(8,128)(2,1)}, u32[]{:S(2)}) copy-start(bf16[256,512]{1,0:T(8,128)(2,1)} %up_ref.1) | copy-start | bytes 786436
  0.0 34.7 %copy-start.4 = (f32[256]{0:T(256)S(1)}, f32[256]{0:T(256)}, u32[]{:S(2)}) copy-start(f32[256]{0:T(256)} %param.19) | copy-start | bytes 3076
  0.0 34.7 %copy-start.3 = (bf16[256,256]{1,0:T(8,128)(2,1)S(1)}, bf16[256,256]{1,0:T(8,128)(2,1)}, u32[]{:S(2)}) copy-start(bf16[256,256]{1,0:T(8,128)(2,1)} %wo_ref.1) | copy-start | bytes 393220
  0.0 34.7 %copy-start = (bf16[8,8,8,256]{3,2,1,0:T(8,128)(2,1)S(1)}, bf16[8,8,8,256]{3,2,1,0:T(8,128)(2,1)}, u32[]{:S(2)}) copy-start(bf16[8,8,8,256]{3,2,1,0:T(8,128)(2,1)} %param.12) | copy-start | bytes 786436

commit v4 on v3

--- a/solution.py
+++ b/solution.py
@@ -15,32 +15,29 @@
 HEADS = 8
 EPSILON = 1e-05
 LOG2E = math.log2(math.e)
+GELU = math.sqrt(2 / math.pi)
 NEG = -1e30
 AHEAD = 3
 
-FACES = [(1, 0, 0), (-1, 0, 0), (0, 1, 0), (0, -1, 0), (0, 0, 1), (0, 0, -1)]
-OTHERS = [
-    (i, j, k)
-    for i in (1, 0, -1)
-    for j in (1, 0, -1)
-    for k in (1, 0, -1)
-    if abs(i) + abs(j) + abs(k) > 1
-]
-DIRS = FACES + OTHERS
-PACKED = 800
+SIGNS = (1, 0, -1)
+ALL = [(i, j, k) for i in SIGNS for j in SIGNS for k in SIGNS if (i, j, k) != (0, 0, 0)]
+ALL.sort(key=lambda d: sum(map(abs, d)))
+NEAR = [d for d in ALL if d[1] == 0]
+FAR = [d for d in ALL if d[1] != 0]
+DIRS = FAR + NEAR
+OWN_AT, SIBLING_AT = (0, 512, 768, 1536), (256, 1024, 1280, 1792)
 SRC = 1024
-MID_AT = 896
+MID_AT = 384
+NEAR_ROWS, FAR_AT, FAR_ROWS = 384, 512, 416
 
 
 def slot(d):
-    if d in FACES:
-        return 80 * FACES.index(d), 80
-    return 512 + 16 * OTHERS.index(d), 16
-
-
-def packed_slot(d):
-    start, rows = slot(d)
-    return (start if start < 512 else start - 32), rows
+    group, at = (NEAR, 0) if d in NEAR else (FAR, FAR_AT)
+    for other in group:
+        rows = 80 if sum(map(abs, other)) == 1 else 16
+        if other == d:
+            return at, rows
+        at += rows
 
 
 AT_Z, AT_M, AT_MZ, KEYS = 800, 1120, 1312, 1408
@@ -118,8 +115,8 @@
     tok_hbm, gain_hbm, wq_hbm, wk_hbm, wv_hbm, scale_hbm, pick_hbm, mask_hbm,
     out_ref,
     nf, mf, tf, cf, stage, packed, src, zbuf, cbuf, abuf, qn, qm, kbuf, vbuf, wbuf, fm, kc, va, held, ms, acc,
-    tok_ref, gain_ref, wq_ref, wk_ref, wv_ref, scale_ref, pick_ref, mask_ref, wvt,
-    load_sem, halo_send, halo_recv, z_send, z_recv, a_send, a_recv, b_send, b_recv, c_send, c_recv,
+    tok_ref, gain_ref, wq_ref, wk_ref, wv_ref, scale_ref, pick_ref, mask_ref, wvt, picked,
+    load_sem, halo_send, halo_recv, far_send, far_recv, z_send, z_recv, a_send, a_recv, b_send, b_recv, c_send, c_recv,
 ):
     loads = [
         pltpu.make_async_copy(a, b, load_sem.at[i])
@@ -172,7 +169,7 @@
     zbuf[0] = (coarse * (1.0 / 64)).astype(BF)
 
     for d in DIRS:
-        start, rows = packed_slot(d)
+        start, rows = slot(d)
         x, y, z = (7 if c > 0 else 0 for c in d)
         mx, my, mz = (3 if c > 0 else 0 for c in d)
         axes = tuple(c != 0 for c in d)
@@ -204,11 +201,11 @@
                 row, mrow = x * 64 + y * 8 + z, mx * 16 + my * 4 + mz
                 stage[c, start : start + 1, :] = nf[c, row : row + 1, :]
                 stage[c, at : at + 1, :] = mf[c, mrow : mrow + 1, :]
-    packed[...] = jnp.concatenate([stage[0], stage[1]], axis=1).astype(BF)
-
-    src[480:512, :] = jnp.zeros((32, 256), BF)
-    src[832:896, :] = jnp.zeros((64, 256), BF)
-    src[960:1024, :] = jnp.zeros((64, 256), BF)
+    for rows in (slice(FAR_AT, FAR_AT + FAR_ROWS), slice(0, NEAR_ROWS)):
+        packed[rows, :] = jnp.concatenate([stage[0, rows, :], stage[1, rows, :]], axis=1).astype(BF)
+
+    src[MID_AT + 64 : FAR_AT, :] = jnp.zeros((FAR_AT - MID_AT - 64, 256), BF)
+    src[FAR_AT + FAR_ROWS : SRC, :] = jnp.zeros((SRC - FAR_AT - FAR_ROWS, 256), BF)
     src[MID_AT : MID_AT + 64, :] = jnp.concatenate([mf[0], mf[1]], axis=1).astype(BF)
 
     pl.semaphore_wait(barrier, len(greeted))
@@ -220,20 +217,19 @@
         )
         for k in range(1, 8)
     ]
-    for copy in z_copies:
-        copy.start()
-    halo = []
+    def message(i, d):
+        rows = pl.ds(*slot(d))
+        pair = (far_send, far_recv) if d in FAR else (halo_send, halo_recv)
+        return pltpu.make_async_remote_copy(
+            src_ref=packed.at[rows], dst_ref=src.at[rows],
+            send_sem=pair[0], recv_sem=pair[1], device_id=near[i], device_id_type=MESH,
+        )
+
     for i, d in enumerate(DIRS):
-        start, rows = packed_slot(d)
-        land, _ = slot(d)
-        halo.append(
-            pltpu.make_async_remote_copy(
-                src_ref=packed.at[pl.ds(start, rows)], dst_ref=src.at[pl.ds(land, rows)],
-                send_sem=halo_send, recv_sem=halo_recv, device_id=near[i], device_id_type=MESH,
-            )
-        )
-    for copy in halo:
-        copy.start()
+        if i == len(FAR):
+            for copy in z_copies:
+                copy.start()
+        message(i, d).start()
 
     for load in loads[2:5]:
         load.wait()
@@ -254,6 +250,22 @@
     ms[...] = jnp.full_like(ms, NEG)
     acc[...] = jnp.zeros_like(acc)
 
+    def wide(rows):
+        return jnp.concatenate([nf[0, rows, :], nf[1, rows, :]], axis=1)
+
+    def project(begin, end):
+        a = abuf[begin:end, :]
+        kbuf[begin:end, :] = dot(a, wk_ref[...]).astype(BF)
+        vbuf[begin:end, :] = dot(a, wv_ref[...]).astype(BF)
+
+    loads[5].wait()
+    for p in range(1, 4):
+        for x in range(8):
+            at = x * 64 + (2 * p - 1) * 8
+            row = (p * 10 + x + 1) * 16
+            abuf[row : row + 16, :] = wide(slice(at, at + 16)).astype(BF)
+        project((p * 10 + 1) * 16, (p * 10 + 9) * 16)
+
     pltpu.make_async_remote_copy(
         src_ref=zbuf.at[pl.ds(1, 7)], dst_ref=zbuf.at[pl.ds(1, 7)], send_sem=z_send, recv_sem=z_recv,
         device_id=along_z[0], device_id_type=MESH,
@@ -269,10 +281,12 @@
     for copy in a_copies:
         copy.start()
 
-    pltpu.make_async_remote_copy(
-        src_ref=packed, dst_ref=packed, send_sem=halo_send, recv_sem=halo_recv,
-        device_id=near[0], device_id_type=MESH,
-    ).wait()
+    def arrived(begin, count, send_sem, recv_sem):
+        rows = pl.ds(begin, count)
+        pltpu.make_async_remote_copy(
+            src_ref=packed.at[rows], dst_ref=src.at[rows], send_sem=send_sem, recv_sem=recv_sem,
+            device_id=near[0], device_id_type=MESH,
+        ).wait()
 
     def cells(d, row):
         start, _ = slot(d)
@@ -281,20 +295,31 @@
         tile = src[low : low + 16, :].astype(F32)
         return tile[at - low : at - low + 8, :]
 
+    for load in loads[6:]:
+        load.wait()
+    arrived(0, NEAR_ROWS, halo_send, halo_recv)
+    for p in range(1, 4):
+        for x, d in ((0, (1, 0, 0)), (9, (-1, 0, 0))):
+            at = (2 * p - 1) * 8
+            row = (p * 10 + x) * 16
+            abuf[row : row + 16, :] = jnp.concatenate([cells(d, at), cells(d, at + 8)], axis=0).astype(BF)
+    picked[...] = dot(pick_ref[:, :FAR_AT], src[0:FAR_AT, :])
+    project(304, 336)
+    project(464, 496)
+
+    arrived(FAR_AT, FAR_ROWS, far_send, far_recv)
     for x in range(10):
         ex = 1 if x == 0 else -1 if x == 9 else 0
         if ex:
-            begin, end = cells((ex, 1, 0), 0), cells((ex, -1, 0), 0)
-            start, _ = slot((ex, 0, 0))
-            inner = src[start : start + 64, :].astype(F32)
+            inner = cells((ex, 0, 0), 0), cells((ex, 0, 0), 56)
+            outer = cells((ex, 1, 0), 0), cells((ex, -1, 0), 0)
         else:
-            begin, end = cells((0, 1, 0), (x - 1) * 8), cells((0, -1, 0), (x - 1) * 8)
-            own = slice((x - 1) * 64, x * 64)
-            inner = jnp.concatenate([nf[0, own, :], nf[1, own, :]], axis=1)
-        abuf[x * 80 : x * 80 + 80, :] = jnp.concatenate([begin, inner, end], axis=0).astype(BF)
-    for load in loads[5:]:
-        load.wait()
-    abuf[AT_Z:KEYS, :] = dot(pick_ref[...], src[...]).astype(BF)
+            at = (x - 1) * 64
+            inner = wide(slice(at, at + 8)), wide(slice(at + 56, at + 64))
+            outer = cells((0, 1, 0), (x - 1) * 8), cells((0, -1, 0), (x - 1) * 8)
+        abuf[x * 16 : x * 16 + 16, :] = jnp.concatenate([outer[0], inner[0]], axis=0).astype(BF)
+        abuf[640 + x * 16 : 656 + x * 16, :] = jnp.concatenate([inner[1], outer[1]], axis=0).astype(BF)
+    abuf[AT_Z:KEYS, :] = (picked[...] + dot(pick_ref[:, FAR_AT:], src[FAR_AT:SRC, :])).astype(BF)
 
     pltpu.make_async_remote_copy(
         src_ref=cbuf.at[pl.ds(64, 192)], dst_ref=cbuf.at[pl.ds(64, 192)], send_sem=a_send, recv_sem=a_recv,
@@ -307,24 +332,19 @@
             send_sem=b_send, recv_sem=b_recv.at[k], device_id=peer, device_id_type=MESH,
         )
 
-    def block(k):
-        return pl.ds(k * 256 if isinstance(k, int) else pl.multiple_of(k * 256, 256), 256)
-
     def swap(k):
         return pltpu.make_async_remote_copy(
-            src_ref=cbuf.at[block(k)], dst_ref=cbuf.at[block(k + 4)],
+            src_ref=cbuf.at[pl.ds(OWN_AT[k], 256)], dst_ref=cbuf.at[pl.ds(SIBLING_AT[k], 256)],
             send_sem=c_send, recv_sem=c_recv.at[k], device_id=partner, device_id_type=MESH,
         )
 
-    ring(0, 256, 256, 1, then[0]).start()
-    ring(0, 512, 256, 2, then[1]).start()
+    ring(0, OWN_AT[1], 256, 1, then[0]).start()
+    ring(0, OWN_AT[2], 256, 2, then[1]).start()
     swap(0).start()
 
-    for i in range(4):
-        rows = slice(i * 352, i * 352 + 352)
-        a = abuf[rows, :]
-        kbuf[rows, :] = dot(a, wk_ref[...]).astype(BF)
-        vbuf[rows, :] = dot(a, wv_ref[...]).astype(BF)
+    project(0, 176)
+    project(624, 1008)
+    project(1008, KEYS)
 
     lane_quad = lax.broadcasted_iota(jnp.int32, (1, 128), 1) // 32
     blank_f, blank_m = jnp.zeros((160, 128), BF), jnp.zeros((96, 128), BF)
@@ -344,7 +364,9 @@
 
         def places(by):
             my = by // 2
-            parts = [rows((2 * bx + i) * 80 + by * 16, 32) for i in range(4)] + [
+            parts = [
+                rows(by * 160 + bx * 32, 64),
+                rows(by * 160 + 160 + bx * 32, 64),
                 rows(AT_Z + by * 80 + bx * 16, 32),
                 rows(AT_M + my * 96 + mx * 32, 64),
                 rows(AT_MZ + my * 48 + mx * 16, 32),
@@ -362,8 +384,8 @@
         def end(unit):
             r0, r1, parts = places(unit // 2)
             lanes = slice(unit % 2 * 128, unit % 2 * 128 + 128)
-            fine = jnp.concatenate([vbuf[p, lanes] for p in parts[:5]] + [blank_m], axis=0)
-            mids = jnp.concatenate([blank_f] + [vbuf[p, lanes] for p in parts[5:]], axis=0)
+            fine = jnp.concatenate([vbuf[p, lanes] for p in parts[:3]] + [blank_m], axis=0)
+            mids = jnp.concatenate([blank_f] + [vbuf[p, lanes] for p in parts[3:]], axis=0)
             left = wbuf[unit, :, 0:128].reshape(16, 8, 128)
             right = wbuf[unit, :, 128:256].reshape(16, 8, 128)
             s0 = (left + mask_ref[:, 0:128][None]).reshape(128, 128)
@@ -392,10 +414,10 @@
 
     lax.fori_loop(0, 4, windows, 0)
 
-    ring(256, 256, 256, 1, then[0]).wait_recv()
-    ring(256, 768, 128, 3, then[0]).start()
-    ring(512, 512, 256, 2, then[1]).wait_recv()
-    ring(640, 896, 128, 3, then[1]).start()
+    ring(0, OWN_AT[1], 256, 1, then[0]).wait_recv()
+    ring(OWN_AT[1], OWN_AT[3], 128, 3, then[0]).start()
+    ring(0, OWN_AT[2], 256, 2, then[1]).wait_recv()
+    ring(OWN_AT[2] + 128, OWN_AT[3] + 128, 128, 3, then[1]).start()
     swap(1).start()
     swap(2).start()
 
@@ -414,20 +436,31 @@
         ms[h] = top
 
     def coarse_block(j, carry):
-        @pl.when(j == 1)
+        @pl.when(j == 0)
         def _():
-            ring(768, 768, 256, 3, then[0]).wait_recv()
+            swap(0).wait_recv()
+
+        @pl.when(j == 2)
+        def _():
+            ring(0, OWN_AT[3], 256, 3, then[0]).wait_recv()
             swap(3).start()
-
-        swap(j).wait_recv()
+            swap(1).wait_recv()
+            swap(2).wait_recv()
+
+        @pl.when(j == 3)
+        def _():
+            swap(3).wait_recv()
+
+        def block(part):
+            return pl.ds(pl.multiple_of(j * 512 + part * 256, 256), 256)
 
         def project_keys(part):
-            k = dot(cbuf[block(j + 4 * part), :], wk_ref[...]).astype(BF)
+            k = dot(cbuf[block(part), :], wk_ref[...]).astype(BF)
             kc[part, 0] = k[:, :128]
             kc[part, 1] = k[:, 128:]
 
         def project_values(part):
-            v = dot_t(wvt[...], cbuf[block(j + 4 * part), :]).astype(BF)
+            v = dot_t(wvt[...], cbuf[block(part), :]).astype(BF)
             for h in range(HEADS):
                 va[part, h, 0:32, :] = v[h * 32 : h * 32 + 32, :]
 
@@ -459,14 +492,21 @@
     ).wait_send()
 
 
-def finish_kernel(att_ref, tok_ref, wo_ref, gain2_ref, up_ref, down_ref, out_ref):
-    for i in range(4):
-        rows = slice(i * 128, i * 128 + 128)
-        residual = (tok_ref[rows, :].astype(F32) + dot(att_ref[rows, :], wo_ref[...])).astype(BF)
+def finish_kernel(att_ref, tok_ref, wo_ref, gain2_ref, up_ref, down_ref, out_hbm, out_ref, sems):
+    parts = [slice(i * 128, i * 128 + 128) for i in range(4)]
+    residuals = [(tok_ref[p, :].astype(F32) + dot(att_ref[p, :], wo_ref[...])).astype(BF) for p in parts]
+    copies = []
+    for i, (p, residual) in enumerate(zip(parts, residuals)):
         wide = residual.astype(F32)
-        second = normalized(wide, gain2_ref[...])
-        hidden = jax.nn.gelu(dot(second, up_ref[...]), approximate=True).astype(BF)
-        out_ref[rows, :] = (wide + dot(hidden, down_ref[...])).astype(BF)
+        u = dot(normalized(wide, gain2_ref[...]), up_ref[...])
+        inner = u * (GELU + (GELU * 0.044715) * (u * u))
+        half = 0.5 * u
+        hidden = (half + half * jnp.tanh(inner)).astype(BF)
+        out_ref[p, :] = (wide + dot(hidden, down_ref[...])).astype(BF)
+        copies.append(pltpu.make_async_copy(out_ref.at[pl.ds(i * 128, 128)], out_hbm.at[pl.ds(i * 128, 128)], sems.at[i]))
+        copies[-1].start()
+    for copy in copies:
+        copy.wait()
 
 
 def shards(
@@ -488,8 +528,8 @@
             V((2, 64, 128), F32),
             V((2, 128, 128), F32),
             V((2, 32, 128), F32),
-            V((2, PACKED, 128), F32),
-            V((PACKED, 256), BF),
+            V((2, SRC, 128), F32),
+            V((SRC, 256), BF),
             V((SRC, 256), BF),
             V((8, 8, 256), BF),
             V((2048, 256), BF),
@@ -514,7 +554,10 @@
             V((KEYS - AT_Z, SRC), BF),
             V((8, 384), F32),
             V((256, 256), BF),
+            V((KEYS - AT_Z, 256), F32),
             dma((8,)),
+            dma,
+            dma,
             dma,
             dma,
             dma,
@@ -549,7 +592,8 @@
         finish_kernel,
         out_shape=jax.ShapeDtypeStruct((512, 256), BF),
         in_specs=[vmem] * 6,
-        out_specs=vmem,
+        out_specs=pl.BlockSpec(memory_space=pl.ANY),
+        scratch_shapes=[V((512, 256), BF), dma((4,))],
         compiler_params=pltpu.CompilerParams(vmem_limit_bytes=12 << 20),
         name="finish",
     )(attended, flat_tokens, out_weight, mlp_gain.reshape(1, 256), up_weight, down_weight)

time: 37.3 us -> 36 us (0.965)
  Pallas kernels: 37.1 us -> 35.6 us
    pallas_call x1, Pallas kernels: 2.53 us -> 1.69 us  [shards(): pl.pallas_call(finish_kernel, out_shape=jax.ShapeDtypeStruct((512, 256),...]
    pallas_call x1, Pallas kernels: 34.6 us -> 33.9 us  [shards(): pl.pallas_call(layer_kernel, out_shape=jax.ShapeDtypeStruct((512, 256), B...]
where the time goes in v4:
time: 36 us; the launch traced here: 35.6 us
  Pallas kernels  35.6 us (99%)
    pallas_call x1, Pallas kernels, shards(): pl.pallas_call(layer_kernel, out_shape=jax.ShapeDtypeStruct((512, 256), B...  33.9 us
    pallas_call x1, Pallas kernels, shards(): pl.pallas_call(finish_kernel, out_shape=jax.ShapeDtypeStruct((512, 256),...  1.69 us

profile of v4, /device:TPU:1, one launch (start us, length us, event | category | flops | bytes accessed | tf_op | source)
XLA Modules:
  0.0 35.6 jit_solution(17208815138430291907)
XLA Ops:
  0.0 0.0 copy-start.2
  0.0 0.0 copy-start.1
  0.0 0.0 copy-start.4
  0.0 0.0 copy-start.3
  0.0 0.0 copy-start
  0.0 33.9 %layer.1.att_ref = bf16[512,256]{1,0:T(8,128)(2,1)S(1)} custom-call(bf16[512,256]{1,0:T(8,128)(2,1)} %bitcast.4, f32[1,256]{1,0:T(1,128)} %bitcast.7, bf16[256,256]{1,0:T(8,128)(2,1)} %wq_hbm.1, bf16[256,256]{1,0:T(8,128)(2,1)} %wk_hbm.1, bf16[256,256]{1,0:T(8,128)(2,1)} %wv_hbm.1, f32[8]{0:T(128)} %scale_hbm.1, bf16[608,1024]{1,0:T(8,128)(2,1)} %constant.4.clone.pick_hbm, ...), custom_call_target="tpu_custom_call" | custom-call | tf_op jit(solution)/shard_map/layer/pallas_call | solution.py:521
  33.9 0.0 copy-done.2
  33.9 0.0 copy-done.1
  33.9 0.0 copy-done.4
  33.9 0.0 copy-done.3
  33.9 0.0 copy-done
  34.0 1.7 %finish.1 = bf16[512,256]{1,0:T(8,128)(2,1)} custom-call(bf16[512,256]{1,0:T(8,128)(2,1)S(1)} %layer.1.att_ref, bf16[512,256]{1,0:T(8,128)(2,1)S(1)} %bitcast.5, bf16[256,256]{1,0:T(8,128)(2,1)S(1)} %copy-done.3, f32[1,256]{1,0:T(1,128)S(1)} %bitcast.6, bf16[256,512]{1,0:T(8,128)(2,1)S(1)} %copy-done.1, bf16[512,256]{1,0:T(8,128)(2,1)S(1)} %copy-done.2), custom_call_target="tpu_custom_call" | custom-call | tf_op jit(solution)/shard_map/finish/pallas_call | solution.py:591
Async XLA Ops:
  0.0 33.9 %copy-start.2 = (bf16[512,256]{1,0:T(8,128)(2,1)S(1)}, bf16[512,256]{1,0:T(8,128)(2,1)}, u32[]{:S(2)}) copy-start(bf16[512,256]{1,0:T(8,128)(2,1)} %down_ref.1) | copy-start | bytes 786436
  0.0 33.9 %copy-start.1 = (bf16[256,512]{1,0:T(8,128)(2,1)S(1)}, bf16[256,512]{1,0:T(8,128)(2,1)}, u32[]{:S(2)}) copy-start(bf16[256,512]{1,0:T(8,128)(2,1)} %up_ref.1) | copy-start | bytes 786436
  0.0 33.9 %copy-start.4 = (f32[256]{0:T(256)S(1)}, f32[256]{0:T(256)}, u32[]{:S(2)}) copy-start(f32[256]{0:T(256)} %param.19) | copy-start | bytes 3076
  0.0 33.9 %copy-start.3 = (bf16[256,256]{1,0:T(8,128)(2,1)S(1)}, bf16[256,256]{1,0:T(8,128)(2,1)}, u32[]{:S(2)}) copy-start(bf16[256,256]{1,0:T(8,128)(2,1)} %wo_ref.1) | copy-start | bytes 393220
  0.0 33.9 %copy-start = (bf16[8,8,8,256]{3,2,1,0:T(8,128)(2,1)S(1)}, bf16[8,8,8,256]{3,2,1,0:T(8,128)(2,1)}, u32[]{:S(2)}) copy-start(bf16[8,8,8,256]{3,2,1,0:T(8,128)(2,1)} %param.12) | copy-start | bytes 786436
